TPU v7x, 32 devices: a whole 2x2x4 slice. The times are simulated.
32 devices in a mesh: fsdp: 8 (over y, x, core), tp: 4 (over z).
Axes of the slice: x: 2, y: 2, z: 4, core: 2. Of those that a mesh axis runs over, the one named last changes fastest.
Arguments:
- pool: bfloat16 [1024, 16384], P(None, 'fsdp'), may hold values from -6 to 6
- ids: int32 [2, 384], replicated, may hold values from 0 to 1023, as said below
- gate_q: bfloat16 [26624, 16384], P(('fsdp', 'tp')), may hold values from -240 to 240, as said below
- up_q: bfloat16 [26624, 16384], P(('fsdp', 'tp')), may hold values from -240 to 240, as said below
- gate_scale: float32 [208, 128], replicated, may hold values from 3e-05 to 0.0003
- up_scale: float32 [208, 128], replicated, may hold values from 3e-05 to 0.0003
- down_weight: bfloat16 [26624, 16384], P('tp', 'fsdp'), may hold values from -0.0390625 to 0.0390625
Outputs:
- mixed: bfloat16 [2, 384, 16384], P(None, 'tp', 'fsdp')
Inputs may be any that keep to these rules, and one draw needn't show every extreme that they name: All 768 ids are different: no request is decoded twice. `gate_q`: every entry is a value of the 8-bit float form e4m3: a sign times (1 + k / 8) times 2 to the power e, with whole k of 0 to 7 and whole e of 0 to 7. `up_q`: every entry is a value of the 8-bit float form e4m3: a sign times (1 + k / 8) times 2 to the power e, with whole k of 0 to 7 and whole e of 0 to 7.
All inputs are finite; a program needn't handle non-finite values.
Results may differ from a plain program's by a relative error of at most 0.0065.
Values may be sent and summed in bfloat16 or wider, within the bound.
No kernel may reach another device: no remote copies, remote signals or barrier semaphores. Data moves between devices by JAX's collectives and lax.ppermute only.
A program may use at most 448 MiB of HBM per device.

v0:
```python
import jax
import jax.numpy as jnp
from jax import lax
from jax.sharding import PartitionSpec as P

BLOCK = 128


def broadcast(block, axis, owner):
    block = jnp.where(lax.axis_index(axis) == owner, block, jnp.zeros_like(block))
    return lax.psum(block, axis)


def project(hidden, down_weight):
    summed = lax.psum_scatter(
        jnp.dot(hidden, down_weight, preferred_element_type=jnp.float32),
        "tp",
        scatter_dimension=0,
        tiled=True,
    )
    return summed.astype(jnp.bfloat16)


def on_device(pool, ids, gate_q, up_q, gate_scale, up_scale, down_weight):
    n_fsdp = lax.axis_size("fsdp")
    n_tp = lax.axis_size("tp")
    fsdp_index = lax.axis_index("fsdp")
    tp_index = lax.axis_index("tp")
    scales = jnp.stack([gate_scale, up_scale])
    steps = ids.shape[0]
    results = []
    quant = jnp.stack([gate_q, up_q])
    rows_here = quant.shape[1]
    width = quant.shape[2]
    owner = fsdp_index * n_tp + tp_index
    row_blocks = (owner * rows_here + jnp.arange(rows_here, dtype=jnp.int32)) // BLOCK
    row_scales = jnp.take(scales, row_blocks, axis=1)
    weights = (
        (
            quant.astype(jnp.float32).reshape(2, rows_here, width // BLOCK, BLOCK)
            * row_scales[:, :, :, None]
        )
        .astype(jnp.bfloat16)
        .reshape(2, rows_here, width)
    )
    group = n_fsdp // n_tp
    for step in range(steps):
        tokens = jnp.take(pool, ids[step], axis=0)
        columns = weights
        both = jnp.einsum(
            "rd,gfd->rgf",
            lax.all_gather(tokens, "fsdp", axis=1, tiled=True),
            columns,
            preferred_element_type=jnp.float32,
        )
        hidden_own = (jax.nn.silu(both[:, 0]) * both[:, 1]).astype(jnp.bfloat16)
        grouped = lax.all_gather(hidden_own, "tp", axis=1, tiled=True)
        columns = []
        for member in range(group):
            columns.append(broadcast(grouped, "fsdp", group * tp_index + member))
        hidden = jnp.concatenate(columns, axis=1)
        results.append(project(hidden, down_weight))
    return jnp.stack(results)


def solution(mesh):
    in_specs = (
        P(None, "fsdp"),
        P(),
        P(("fsdp", "tp"), None),
        P(("fsdp", "tp"), None),
        P(),
        P(),
        P("tp", "fsdp"),
    )
    out_specs = P(None, "tp", "fsdp")
    return jax.shard_map(
        on_device, mesh=mesh, in_specs=in_specs, out_specs=out_specs, check_vma=False
    )
```

profile of v0, /device:TPU:0, one launch (start us, length us, event | category | flops | bytes accessed | tf_op | source)
XLA Modules:
  0.0 666.3 jit_solution(9128246473485798060)
XLA Ops:
  6.5 0.0 all-gather.5.cloned.1.call-start
  6.5 0.8 slice_reduce_fusion.1
  7.4 7.1 %gather_fusion.1 = bf16[384,2048]{1,0:T(8,128)(2,1)S(1)} fusion(bf16[1024,2048]{1,0:T(8,128)(2,1)} %param.9, s32[1024]{0:T(1024)S(1)} %pad_clamp_fusion.2), kind=kCustom, calls=%fused_computation.clone | custom fusion | bytes 3147264 | tf_op jit(solution)/shard_map/jit(_take)/gather | solution.py:48
  14.5 1.4 broadcast_select_fusion.5
  15.9 0.0 all-gather.5.cloned.1.call-update
  15.9 0.0 all-gather.9.cloned.1.call-start
  16.0 7.1 %gather_fusion.2 = bf16[384,2048]{1,0:T(8,128)(2,1)S(1)} fusion(bf16[1024,2048]{1,0:T(8,128)(2,1)} %param.9, s32[1024]{0:T(1024)S(1)} %pad_clamp_fusion), kind=kCustom, calls=%fused_computation.1.clone | custom fusion | bytes 3147264 | tf_op jit(solution)/shard_map/jit(_take)/gather | solution.py:48
  23.1 0.0 copy-start
  23.1 0.0 copy-start.1
  23.1 1.4 broadcast_select_fusion.4
  24.5 0.0 all-gather.9.cloned.1.call-update
  24.5 0.2 all-gather.7.cloned.1.call-start
  24.8 0.0 copy-done
  24.8 0.0 copy-done.1
  24.9 0.2 pad_maximum_fusion.1
  25.1 3.5 gather_fusion
  28.6 3.1 select_bitcast_fusion
  31.7 0.1 copy.8
  31.7 37.6 %mul.39 = f32[2,832,128,128]{3,2,1,0:T(8,128)} broadcast(f32[2,832,128]{2,1,0:T(8,128)S(1)} %copy.8), dimensions={0,1,2} | broadcast | bytes 109903872 | tf_op jit(solution)/shard_map/mul | solution.py:40
  69.3 116.0 %mul.40 = f32[2,832,16384]{2,1,0:T(8,128)} reshape(f32[2,832,128,128]{3,2,1,0:T(8,128)} %mul.39) | data formatting | bytes 218103808 | tf_op jit(solution)/shard_map/mul | solution.py:40
  185.2 0.0 all-gather.5.cloned.1.call-done
  185.2 60.5 %fusion.2 = f32[384,2,832]{0,2,1:T(8,128)S(1)} fusion(bf16[384,16384]{1,0:T(8,128)(2,1)} %all-gather.5.cloned.1.call-done, f32[2,832,16384]{2,1,0:T(8,128)} %mul.40, bf16[1,832,16384]{2,1,0:T(8,128)(2,1)} %bitcast.42, bf16[1,832,16384]{2,1,0:T(8,128)(2,1)} %bitcast.44), kind=kOutput, calls=%fused_computation.6 | convolution fusion | flops 21101543424 | bytes 178716672 | tf_op jit(solution)/shard_map/rd,gfd->rgf/dot_general | solution.py:50
  245.7 1.2 fusion.15
  247.0 0.0 all-gather.7.cloned.1.call-update
  247.0 0.0 all-gather.11.cloned.1.call-start
  247.0 0.0 all-gather.9.cloned.1.call-done
  247.1 61.2 %fusion = f32[384,2,832]{0,2,1:T(8,128)S(1)} fusion(bf16[384,16384]{1,0:T(8,128)(2,1)} %all-gather.9.cloned.1.call-done, f32[2,832,16384]{2,1,0:T(8,128)} %mul.40, bf16[1,832,16384]{2,1,0:T(8,128)(2,1)} %bitcast.43, bf16[1,832,16384]{2,1,0:T(8,128)(2,1)} %bitcast.45), kind=kOutput, calls=%fused_computation.4 | convolution fusion | flops 21101543424 | bytes 178716672 | tf_op jit(solution)/shard_map/rd,gfd->rgf/dot_general | solution.py:50
  308.2 1.2 fusion.13
  309.4 0.0 all-gather.11.cloned.1.call-update
  309.5 0.3 all-reduce.3.cloned.1.call-start
  309.7 0.0 all-gather.7.cloned.1.call-done
  309.8 4.5 broadcast_select_fusion.3
  314.3 51.8 %all-gather.11.cloned.1.call-done = bf16[384,3328]{0,1:T(8,128)(2,1)} async-done(((bf16[384,832]{0,1:T(8,128)(2,1)}), bf16[384,3328]{0,1:T(8,128)(2,1)}) %all-gather.11.cloned.1.call-update) | async-done | bytes 2555920 | tf_op jit(solution)/shard_map/all_gather | solution.py:57
  366.0 4.4 broadcast_select_fusion.2
  370.4 0.0 all-reduce.3.cloned.1.call-update
  370.4 0.0 reduce-scatter.3.cloned.1.call-start
  370.5 145.1 %all-reduce.3.cloned.1.call-done = (bf16[384,3328]{0,1:T(8,128)(2,1)}, bf16[384,3328]{0,1:T(8,128)(2,1)}, bf16[384,3328]{0,1:T(8,128)(2,1)}, bf16[384,3328]{0,1:T(8,128)(2,1)}) async-done(((bf16[384,3328]{0,1:T(8,128)(2,1)}, bf16[384,3328]{0,1:T(8,128)(2,1)}, bf16[384,3328]{0,1:T(8,128)(2,1)}, bf16[384,3328]{0,1:T(8,128)(2,1)}), (bf16[384,3328]{0,1:T(8,128)(2,1)}, bf16[384,3328]{0,1:T(8,128)(2,1)}, ...) | async-done | bytes 10223632 | tf_op jit(solution)/shard_map/psum | solution.py:11
  515.6 18.4 %fusion.4 = f32[384,2048]{1,0:T(8,128)} fusion(bf16[6656,2048]{1,0:T(8,128)(2,1)} %param.15, bf16[384,3328]{0,1:T(8,128)(2,1)} %get-tuple-element.10, bf16[384,3328]{0,1:T(8,128)(2,1)} %get-tuple-element.11), kind=kOutput, calls=%fused_computation.8 | convolution fusion | flops 10479206400 | bytes 35520512 | tf_op jit(solution)/shard_map/dot_general | solution.py:16
  534.0 0.0 reduce-scatter.3.cloned.1.call-update
  534.0 0.0 reduce-scatter.5.cloned.1.call-start
  534.1 1.6 copy-done.2
  535.7 18.3 %fusion.8 = f32[384,2048]{1,0:T(8,128)} fusion(bf16[6656,2048]{1,0:T(8,128)(2,1)} %param.15, bf16[384,3328]{0,1:T(8,128)(2,1)S(1)} %copy-done.2, bf16[384,3328]{0,1:T(8,128)(2,1)} %get-tuple-element.9), kind=kOutput, calls=%fused_computation.12 | convolution fusion | flops 10479206400 | bytes 35520512 | tf_op jit(solution)/shard_map/dot_general | solution.py:16
  554.0 0.0 reduce-scatter.5.cloned.1.call-update
  554.0 40.6 %reduce-scatter.3.cloned.1.call-done = f32[96,2048]{1,0:T(8,128)} async-done(((f32[384,2048]{1,0:T(8,128)}), f32[96,2048]{1,0:T(8,128)}) %reduce-scatter.3.cloned.1.call-update) | async-done | bytes 786448 | tf_op jit(solution)/shard_map/reduce_scatter | solution.py:15
  594.7 1.2 convert_bitcast_fusion.1
  595.9 61.5 %reduce-scatter.5.cloned.1.call-done = f32[96,2048]{1,0:T(8,128)} async-done(((f32[384,2048]{1,0:T(8,128)}), f32[96,2048]{1,0:T(8,128)}) %reduce-scatter.5.cloned.1.call-update) | async-done | bytes 786448 | tf_op jit(solution)/shard_map/reduce_scatter | solution.py:15
  657.3 1.2 convert_bitcast_fusion
  658.5 0.9 pad_maximum_fusion
  (10 shorter events, 0.1 us)
Async XLA Ops:
  6.5 178.7 %all-gather.5.cloned.1.call-start = ((), (), s32[]{:S(2)}) async-start(), calls=%async_computation.2 | async-start | bytes 14155776 | tf_op jit(solution)/shard_map/all_gather | solution.py:52
  15.9 231.2 %all-gather.9.cloned.1.call-start = ((), (), s32[]{:S(2)}) async-start(), calls=%async_computation.5 | async-start | bytes 14155776 | tf_op jit(solution)/shard_map/all_gather | solution.py:52
  23.1 1.8 copy-start
  23.1 1.7 copy-start.1
  24.5 285.2 %all-gather.7.cloned.1.call-start = ((), (), s32[]{:S(2)}) async-start(), calls=%async_computation.3 | async-start | bytes 3194880 | tf_op jit(solution)/shard_map/all_gather | solution.py:57
  247.0 119.0 %all-gather.11.cloned.1.call-start = ((), (), s32[]{:S(2)}) async-start(), calls=%async_computation.6 | async-start | bytes 3194880 | tf_op jit(solution)/shard_map/all_gather | solution.py:57
  309.5 206.2 %all-reduce.3.cloned.1.call-start = ((), (), s32[]{:S(2)}) async-start(), calls=%async_computation.8 | async-start | bytes 20447232 | tf_op jit(solution)/shard_map/psum | solution.py:11
  370.4 224.2 %reduce-scatter.3.cloned.1.call-start = ((), (), s32[]{:S(2)}) async-start(), calls=%async_computation.4 | async-start | bytes 3932160 | tf_op jit(solution)/shard_map/reduce_scatter | solution.py:15
  534.0 1.7 copy-start.2
  534.0 123.3 %reduce-scatter.5.cloned.1.call-start = ((), (), s32[]{:S(2)}) async-start(), calls=%async_computation.7 | async-start | bytes 3932160 | tf_op jit(solution)/shard_map/reduce_scatter | solution.py:15
Sparse Core Ops, SparseCore 0:
  16.0 74.7 all-gather.4
  92.7 71.9 all-gather.8
  247.1 56.3 all-gather.6
  309.6 56.3 all-gather.10
  370.6 144.9 all-reduce.2
  534.2 60.4 reduce-scatter.2
  597.0 60.3 reduce-scatter.4
where the time goes:
time: 670 us; the launch traced here: 666 us
  waiting for transfers between devices  299 us (45%)
  local copies, waits for them, and re-layouts  174 us (26%)
  matrix products  158 us (24%)
  other arithmetic  20.7 us (3%)
  between operations  13.7 us (2%)
    mul x2, local copies, waits for them, and re-layouts, on_device(): quant.astype(jnp.float32).reshape(2, rows_here, width // BLOCK, BLOCK)  154 us
    psum x1, waiting for transfers between devices, broadcast(): return lax.psum(block, axis)  145 us
    dot_general x2, matrix products, on_device(): jnp.einsum('rd,gfd->rgf', lax.all_gather(tokens, 'fsdp', axis=1, tiled=Tr...  122 us
    reduce_scatter x2, waiting for transfers between devices, project(): lax.psum_scatter(jnp.dot(hidden, down_weight, preferred_element_type=jnp....  102 us
    all_gather x2, waiting for transfers between devices, on_device(): grouped = lax.all_gather(hidden_own, 'tp', axis=1, tiled=True)  51.8 us
    dot_general x2, matrix products, project(): jnp.dot(hidden, down_weight, preferred_element_type=jnp.float32)  36.7 us
    gather x2, local copies, waits for them, and re-layouts, on_device(): tokens = jnp.take(pool, ids[step], axis=0)  14.2 us
  transfers between devices with their start and end apart: 7, of which 4 were waited for; matrix products, arithmetic and copies ran while one was open for 48% of the time, Pallas kernels for 0%

commit v1 on v0

v1 whole, which is shorter than its diff:
```python
import functools
import math

import jax
import jax.numpy as jnp
from jax import lax
from jax.experimental import pallas as pl
from jax.experimental.pallas import tpu as pltpu
from jax.experimental.layout import Layout, with_layout_constraint
from jax.sharding import PartitionSpec as P

BLOCK = 128
HALVES = 2
LANES = 128
VMEM_BYTES = 32 << 20
CHUNKS = (2, 1)


def rows_first(x):
    return with_layout_constraint(x, Layout(major_to_minor=tuple(range(x.ndim))))


def swap(block, mask):
    n = lax.axis_size("fsdp")
    moved = lax.ppermute(rows_first(block), "fsdp", [(i, i ^ mask) for i in range(n)])
    return rows_first(moved)


def shift(block, by):
    n = lax.axis_size("tp")
    moved = lax.ppermute(rows_first(block), "tp", [(i, (i + by) % n) for i in range(n)])
    return rows_first(moved)


def after(values, *others):
    return lax.optimization_barrier((values, others))[0]


def flips():
    masks, bit = [], 2
    while bit < lax.axis_size("fsdp"):
        masks.append(bit)
        bit *= 2
    return masks


def last_flips(mask):
    flip_list = flips()
    routes = []
    for i in range(HALVES):
        turn = i % len(flip_list)
        order = flip_list[turn:] + flip_list[:turn]
        routes.append([d for d in order if d & mask][-1])
    return routes


def levels():
    masks = range(2, lax.axis_size("fsdp"), 2)
    return [[r for r in masks if r.bit_count() == n] for n in range(1, len(flips()) + 1)]


def spread(got, level, axis):
    def part(pieces, i):
        if len(pieces) > 1:
            return pieces[i]
        size = pieces[0].shape[axis] // HALVES
        return lax.slice_in_dim(pieces[0], i * size, (i + 1) * size, axis=axis)

    for r in level:
        if r.bit_count() == 1:
            got[r] = [swap(got[0][0], r)]
        else:
            got[r] = [swap(part(got[r ^ d], i), d) for i, d in enumerate(last_flips(r))]


def other_core(pieces):
    return [swap(p, 1) for p in pieces]


def when_step(step, n, action):
    for i in range(n):

        @pl.when(step == i)
        def _(i=i):
            action(i)


def gate_up_kernel(parts, first, last, g, idx, *refs):
    n = len(parts)
    n_arrays = 1 + max(a for a, _ in parts)
    xs, refs = refs[:n_arrays], refs[n_arrays:]
    gq, uq, gs, us, refs = *refs[:4], refs[4:]
    if not first:
        acc, refs = refs[0], refs[1:]
    if last:
        out, w, xb, sem = refs
    elif first:
        acc, w, xb, sem = refs
    else:
        _, w, xb, sem = refs
    k = pl.program_id(0)
    tk = xb.shape[2]
    rows = gq.shape[0]

    def copy(i):
        a, part = parts[i]
        return pltpu.make_async_copy(
            xs[a].at[:, pl.ds(part * tk, tk)], xb.at[i % 2], sem.at[i % 2]
        )

    @pl.when(k == 0)
    def _():
        copy(0).start()
        if first:
            acc[...] = jnp.zeros_like(acc)

    when_step(k + 1, n, lambda i: copy(i).start())
    slot = lax.rem(k, 2)
    for i, (q, s) in enumerate(((gq, gs), (uq, us))):
        for j in range(rows // g):
            w[i * rows + j * g : i * rows + (j + 1) * g, :] = (
                q[j * g : (j + 1) * g, :].astype(jnp.float32) * s[j : j + 1, :]
            ).astype(jnp.bfloat16)
    pltpu.make_async_copy(
        xs[0].at[:, pl.ds(0, tk)], xb.at[slot], sem.at[slot]
    ).wait()
    acc[...] += lax.dot_general(
        w[...], xb[slot], (((1,), (1,)), ((), ())), preferred_element_type=jnp.float32
    )
    if last:

        @pl.when(k == n - 1)
        def _():
            gate = acc[:rows, :]
            hidden = gate / (1.0 + jnp.exp(-gate)) * acc[rows:, :]
            out[:, :rows] = hidden.T.astype(out.dtype)
            if out.shape[1] > rows:
                out[:, rows:] = jnp.zeros((out.shape[0], out.shape[1] - rows), out.dtype)


def gate_up(tk, arrays, parts, at, columns, weights, acc, last):
    m = arrays[0].shape[0]
    gate_q, _, gate_s, _ = weights
    rows = gate_q.shape[0]
    n = len(parts)
    groups = gate_s.shape[0]
    quant = pl.BlockSpec((rows, tk), lambda k, idx: (0, idx[k + at]))
    scale = pl.BlockSpec((groups, tk), lambda k, idx: (0, idx[k + at]))
    in_specs = [pl.BlockSpec(memory_space=pl.ANY)] * len(arrays)
    in_specs += [quant, quant, scale, scale]
    operands = [*arrays, *weights]
    aliases = {}
    if acc is not None:
        in_specs.append(pl.BlockSpec(memory_space=pltpu.VMEM))
        operands.append(acc)
        if not last:
            aliases = {len(operands): 0}
    scratch = [
        pltpu.VMEM((2 * rows, tk), jnp.bfloat16),
        pltpu.VMEM((2, m, tk), jnp.bfloat16),
        pltpu.SemaphoreType.DMA((2,)),
    ]
    if last:
        padded = pl.cdiv(rows, LANES) * LANES
        out_specs = pl.BlockSpec((m, padded), lambda k, idx: (0, 0))
        out_shape = jax.ShapeDtypeStruct((m, padded), jnp.bfloat16)
    else:
        out_specs = pl.BlockSpec(memory_space=pltpu.VMEM)
        out_shape = jax.ShapeDtypeStruct((2 * rows, m), jnp.float32)
    return pl.pallas_call(
        functools.partial(gate_up_kernel, parts, acc is None, last, rows // groups),
        grid_spec=pltpu.PrefetchScalarGridSpec(
            num_scalar_prefetch=1,
            grid=(n,),
            in_specs=in_specs,
            out_specs=out_specs,
            scratch_shapes=scratch,
        ),
        out_shape=out_shape,
        input_output_aliases=aliases,
        cost_estimate=pl.CostEstimate(
            flops=4 * m * rows * tk * n,
            bytes_accessed=4 * rows * tk * n,
            transcendentals=0,
        ),
        compiler_params=pltpu.CompilerParams(
            dimension_semantics=("arbitrary",), vmem_limit_bytes=VMEM_BYTES
        ),
    )(columns, *operands)


def down_kernel(sources, n_tp, idx, *refs):
    n_arrays = 1 + max(a for parts in sources for a, _ in parts)
    xs, (dw, out, acc, xb, sem) = refs[:n_arrays], refs[n_arrays:]
    n = len(sources)
    members = len(sources[0])
    pm = xb.shape[1] // members
    rr = pm // n_tp
    k = pl.program_id(0)

    def start(i):
        for r, (a, row) in enumerate(sources[i]):
            pltpu.make_async_copy(
                xs[a].at[pl.ds(row, pm), :],
                xb.at[i % 2, pl.ds(r * pm, pm), :],
                sem.at[i % 2, r],
            ).start()

    @pl.when(k == 0)
    def _():
        start(0)
        acc[...] = jnp.zeros_like(acc)

    when_step(k + 1, n, start)
    slot = lax.rem(k, 2)
    for r in range(members):
        pltpu.make_async_copy(
            xs[0].at[pl.ds(0, pm), :], xb.at[slot, pl.ds(r * pm, pm), :], sem.at[slot, r]
        ).wait()
    acc[...] += jnp.dot(
        xb[slot, :, : dw.shape[0]], dw[...], preferred_element_type=jnp.float32
    )

    @pl.when(k == n - 1)
    def _():
        for to in range(n_tp):
            for r in range(members):
                a, b = r * pm + to * rr, (to * members + r) * rr
                out[b : b + rr, :] = acc[a : a + rr, :].astype(out.dtype)


def down(n_tp, rows, arrays, sources, pm, chunks, down_weight):
    padded = arrays[0].shape[1]
    m = pm * len(sources[0])
    width = down_weight.shape[1]
    n = len(sources)
    return pl.pallas_call(
        functools.partial(down_kernel, sources, n_tp),
        grid_spec=pltpu.PrefetchScalarGridSpec(
            num_scalar_prefetch=1,
            grid=(n,),
            in_specs=[pl.BlockSpec(memory_space=pl.ANY)] * len(arrays)
            + [pl.BlockSpec((rows, width), lambda k, idx: (idx[k], 0))],
            out_specs=pl.BlockSpec((m, width), lambda k, idx: (0, 0)),
            scratch_shapes=[
                pltpu.VMEM((m, width), jnp.float32),
                pltpu.VMEM((2, m, padded), jnp.bfloat16),
                pltpu.SemaphoreType.DMA((2, len(sources[0]))),
            ],
        ),
        out_shape=jax.ShapeDtypeStruct((m, width), jnp.bfloat16),
        cost_estimate=pl.CostEstimate(
            flops=2 * m * rows * width * n,
            bytes_accessed=2 * rows * width * n,
            transcendentals=0,
        ),
        compiler_params=pltpu.CompilerParams(
            dimension_semantics=("arbitrary",), vmem_limit_bytes=VMEM_BYTES
        ),
    )(chunks, *arrays, down_weight)


def on_device(pool, ids, gate_q, up_q, gate_scale, up_scale, down_weight):
    n_fsdp = lax.axis_size("fsdp")
    n_tp = lax.axis_size("tp")
    f = lax.axis_index("fsdp")
    t = lax.axis_index("tp")
    rows_here = gate_q.shape[0]
    width = pool.shape[1]
    steps, step_rows = ids.shape
    members = n_fsdp // 2
    spans = n_fsdp // n_tp // 2
    q = f // 2
    core = f % 2
    near = levels()
    masks = [0] + [r for level in near for r in level]

    g = math.gcd(rows_here, BLOCK)
    row_blocks = (
        (f * n_tp + t) * rows_here + g * jnp.arange(rows_here // g, dtype=jnp.int32)
    ) // BLOCK
    weights = (gate_q, up_q) + tuple(
        jnp.repeat(jnp.take(s, row_blocks, axis=0), BLOCK, axis=1)
        for s in (gate_scale, up_scale)
    )

    share = steps * step_rows // n_tp
    by_owner = ids.reshape(steps, n_tp, step_rows // n_tp).transpose(1, 0, 2)
    by_owner = by_owner.reshape(n_tp, share)
    requests = jnp.arange(pool.shape[0], dtype=jnp.int32)

    def pick(begin, end):
        rr = (end - begin) // members
        named = by_owner[:, begin:end].reshape(n_tp, members, rr).transpose(1, 0, 2)
        chosen = (named.reshape(-1, 1) == requests).astype(jnp.bfloat16)
        picked = jnp.dot(chosen, pool, preferred_element_type=jnp.float32)
        return picked.astype(jnp.bfloat16)

    halves = jnp.arange(HALVES, dtype=jnp.int32)

    def columns_of(masks_in_order):
        flipped = f ^ jnp.array(masks_in_order, dtype=jnp.int32)
        return (flipped[:, None] * HALVES + halves).reshape(-1)

    visits = [0, 1]
    for c in range(2):
        visits += [r ^ c for r in near[0]]
    for c in range(2):
        visits += [r ^ c for level in near[1:] for r in level]
    columns = columns_of(visits)

    def gate_up_part(wanted, acc, last):
        arrays, parts = [], []
        for r, c, pieces in wanted:
            for p in pieces:
                for j in range(HALVES // len(pieces)):
                    parts.append((len(arrays), j))
                arrays.append(p)
        r, c, _ = wanted[0]
        at = visits.index(r ^ c) * HALVES
        return gate_up(
            width // HALVES, arrays, tuple(parts), at, columns, weights, acc, last
        )

    def scatter(hidden):
        pm = hidden.shape[0] // members
        pieces = [
            lax.dynamic_slice_in_dim(hidden, (q ^ (r // 2)) * pm, pm, axis=0)
            for r in range(0, n_fsdp, 2)
        ]
        return [swap(p, 2 * i) if i else p for i, p in enumerate(pieces)]

    def to_planes(pieces):
        pieces = jnp.stack(pieces)
        arrived = []
        for dz in range(n_tp):
            to = (t + dz) % n_tp
            for v in range(spans):
                piece = lax.dynamic_index_in_dim(
                    pieces, q ^ (to * spans + v), 0, keepdims=False
                )
                arrived.append(shift(piece, dz) if dz else piece)
        return arrived

    def down_part(by_core):
        n_here = n_tp * spans
        pm = by_core[0][0][0].shape[0] // n_here
        arrays, where, sources, chunks = [], {}, [], []
        for c, got in enumerate(by_core):
            for r in masks:
                where[c, r] = (len(arrays), len(got[r]))
                arrays.extend(got[r])
        for c in range(2):
            for i in range(n_here):
                parts = []
                for r in masks:
                    a, held = where[c, r]
                    each = n_here // held
                    parts.append((a + i // each, (i % each) * pm))
                sources.append(tuple(parts))
                dz, v = divmod(i, spans)
                chunks.append((2 * v + (core ^ c)) * n_tp + (t - dz) % n_tp)
        chunks = jnp.stack(chunks).astype(jnp.int32)
        return down(n_tp, rows_here, arrays, tuple(sources), pm, chunks, down_weight)

    def exchange(partial):
        rows = partial.shape[0] // n_tp
        shares = [
            lax.dynamic_slice_in_dim(partial, (t + dz) % n_tp * rows, rows, axis=0)
            for dz in range(n_tp)
        ]
        return [shift(s, dz) if dz else s for dz, s in enumerate(shares)]

    def total(shares):
        summed = functools.reduce(jnp.add, [s.astype(jnp.float32) for s in shares])
        rr = summed.shape[0] // members
        summed = summed.astype(jnp.bfloat16).reshape(members, rr, width)
        place = {r: i for i, r in enumerate(masks)}
        back = jnp.array([place[2 * i] for i in range(members)], dtype=jnp.int32)
        ordered = [
            lax.dynamic_index_in_dim(summed, back[q ^ i], 0, keepdims=False)
            for i in range(members)
        ]
        return jnp.concatenate(ordered)

    n = len(CHUNKS)
    ends = [share * sum(CHUNKS[: i + 1]) // sum(CHUNKS) for i in range(n)]
    own = [pick(b, e) for b, e in zip([0] + ends[:-1], ends)]
    tokens = [{0: [x]} for x in own]

    far = [r for level in near[1:] for r in level]

    def blocks_of(got, group):
        return [got[r] for r in group]

    def hold(got, group, *others):
        for r, held in zip(group, after(blocks_of(got, group), *others)):
            got[r] = held

    def far_blocks(got, axis):
        for level in near[1:]:
            spread(got, level, axis)

    def land(pieces):
        got = {0: [jnp.concatenate(pieces)]}
        spread(got, near[0], 0)
        return got

    def twins_of(got, group):
        return {r: other_core(got[r]) for r in group}

    def hold_all(pieces, *others):
        held = after([p for _, _, p in pieces], *others)
        return [(r, c, p) for (r, c, _), p in zip(pieces, held)]

    def wanted(got, core_flip, group):
        return [(r, core_flip, got[r]) for r in group]

    first, last = tokens

    spread(first, near[0], 1)
    here = [wanted(x, 0, [0]) + wanted(twins_of(x, [0]), 1, [0]) for x in tokens]
    acc_first = gate_up_part(here[0], None, False)
    acc_last = gate_up_part(hold_all(here[1], acc_first), None, False)

    hold(first, near[0], acc_last)
    far_blocks(first, 1)
    twins = twins_of(first, near[0])
    last[0] = after(last[0], blocks_of(first, near[0]))
    spread(last, near[0], 1)
    acc_first = gate_up_part(wanted(first, 0, near[0]), acc_first, False)
    acc_first = gate_up_part(wanted(twins, 1, near[0]), acc_first, False)
    hold(first, far, acc_first)
    pieces = wanted(first, 0, far) + wanted(twins_of(first, far), 1, far)
    hidden_first = gate_up_part(pieces, acc_first, True)
    moved_first = scatter(hidden_first)

    hold(last, near[0], hidden_first)
    far_blocks(last, 1)
    twins = twins_of(last, near[0])
    moved_first = to_planes(after(moved_first, blocks_of(last, near[0])))
    pieces = wanted(last, 0, near[0]) + wanted(twins, 1, near[0])
    acc_last = gate_up_part(hold_all(pieces, moved_first[0]), acc_last, False)
    hold(last, far, acc_last)
    twins = twins_of(last, far)
    landed_first = land(after(moved_first, acc_last))
    pieces = wanted(last, 0, far) + wanted(twins, 1, far)
    hidden_last = gate_up_part(pieces, acc_last, True)
    moved_last = scatter(hidden_last)

    hold(landed_first, near[0], hidden_last)
    far_blocks(landed_first, 0)
    twins = twins_of(landed_first, [0] + near[0])
    moved_last = to_planes(after(moved_last, blocks_of(landed_first, near[0])))
    twins.update(twins_of(landed_first, far))
    partial_first = down_part((landed_first, twins))
    shares_first = exchange(partial_first)
    landed_last = land(after(moved_last, shares_first[0]))

    hold(landed_last, near[0], partial_first)
    far_blocks(landed_last, 0)
    twins = twins_of(landed_last, masks)
    partial_last = down_part((landed_last, twins))
    shares_last = exchange(partial_last)
    shares_first, shares_last = after((shares_first, shares_last))
    mixed = [total(shares_first), total(shares_last)]
    return jnp.concatenate(mixed).reshape(steps, share // steps, width)


def solution(mesh):
    in_specs = (
        P(None, "fsdp"),
        P(),
        P(("fsdp", "tp"), None),
        P(("fsdp", "tp"), None),
        P(),
        P(),
        P("tp", "fsdp"),
    )
    out_specs = P(None, "tp", "fsdp")

    return jax.shard_map(
        on_device, mesh=mesh, in_specs=in_specs, out_specs=out_specs, check_vma=False
    )
```

time: 670 us -> 335 us (0.50)
  waiting for transfers between devices: 299 us -> 94.4 us
  local copies, waits for them, and re-layouts: 174 us -> 20.6 us
  matrix products: 158 us -> 10.4 us
  Pallas kernels: 0 us -> 143 us
  starting transfers between devices: 0.65 us -> 60.5 us
  other arithmetic: 20.7 us -> 4.5 us
  between operations: 13.7 us -> 0.53 us
    mul x2 -> x0, local copies, waits for them, and re-layouts: 154 us -> none  [on_device(): quant.astype(jnp.float32).reshape(2, rows_here, width // BLOCK, BLOCK)]
    dot_general x4 -> x2, matrix products: 158 us -> 10.4 us  [pick(): picked = jnp.dot(chosen, pool, preferred_element_type=jnp.float32)]
    psum x1 -> x0, waiting for transfers between devices: 145 us -> none  [broadcast(): return lax.psum(block, axis)]
    pallas_call x0 -> x9, Pallas kernels: none -> 143 us  [the longest x7 97.3 us: gate_up(): pl.pallas_call(functools.partial(gate_up_kernel, parts, acc is None, last...]
    reduce_scatter x2 -> x0, waiting for transfers between devices: 102 us -> none  [project(): lax.psum_scatter(jnp.dot(hidden, down_weight, preferred_element_type=jnp....]
    ppermute x0 -> x54, waiting for transfers between devices: none -> 94.4 us  [the longest x42 61.8 us: swap(): lax.ppermute(rows_first(block), 'fsdp', [(i, i ^ mask) for i in range(n)])]
    ppermute x0 -> x54, starting transfers between devices: none -> 60.5 us  [the longest x42 30.4 us: swap(): lax.ppermute(rows_first(block), 'fsdp', [(i, i ^ mask) for i in range(n)])]
    all_gather x4 -> x0, waiting for transfers between devices: 51.8 us -> none  [the longest x2 51.8 us: on_device(): grouped = lax.all_gather(hidden_own, 'tp', axis=1, tiled=True)]
  transfers between devices with their start and end apart: 7 -> 54, of which waited for: 4 -> 17; matrix products, arithmetic and copies ran while one was open for 48% -> 7% of each run, Pallas kernels for 0% -> 43%
where the time goes in v1:
time: 335 us; the launch traced here: 334 us
  Pallas kernels  143 us (43%)
  waiting for transfers between devices  94.4 us (28%)
  starting transfers between devices  60.5 us (18%)
  local copies, waits for them, and re-layouts  20.6 us (6%)
  matrix products  10.4 us (3%)
  other arithmetic  4.5 us (1%)
    pallas_call x7, Pallas kernels, gate_up(): pl.pallas_call(functools.partial(gate_up_kernel, parts, acc is None, last...  97.3 us
    ppermute x42, waiting for transfers between devices, swap(): lax.ppermute(rows_first(block), 'fsdp', [(i, i ^ mask) for i in range(n)])  61.8 us
    pallas_call x2, Pallas kernels, down(): pl.pallas_call(functools.partial(down_kernel, sources, n_tp), grid_spec=p...  46.1 us
    ppermute x12, waiting for transfers between devices, shift(): lax.ppermute(rows_first(block), 'tp', [(i, (i + by) % n) for i in range(n)])  32.6 us
    ppermute x42, starting transfers between devices, swap(): lax.ppermute(rows_first(block), 'fsdp', [(i, i ^ mask) for i in range(n)])  30.4 us
    ppermute x12, starting transfers between devices, shift(): lax.ppermute(rows_first(block), 'tp', [(i, (i + by) % n) for i in range(n)])  30.1 us
    dot_general x2, matrix products, pick(): picked = jnp.dot(chosen, pool, preferred_element_type=jnp.float32)  10.4 us
    unnamed x35, local copies, waits for them, and re-layouts  7.25 us
  transfers between devices with their start and end apart: 54, of which 17 were waited for; matrix products, arithmetic and copies ran while one was open for 7% of the time, Pallas kernels for 43%

profile of v1, /device:TPU:0, one launch (start us, length us, event | category | flops | bytes accessed | tf_op | source)
XLA Modules:
  0.0 334.4 jit_solution(8840814662721414496)
XLA Ops:
  1.1 5.9 %convolution_convert_fusion.refs_0_ = bf16[512,2048]{1,0:T(8,128)(2,1)} fusion(bf16[1024,2048]{1,0:T(8,128)(2,1)} %param.12, s32[512]{0:T(512)S(1)} %eq.64), kind=kOutput, calls=%fused_computation.2 | convolution fusion | flops 2149056512 | bytes 6293504 | tf_op jit(solution)/shard_map/dot_general | solution.py:296
  7.5 2.5 collective-permute-start.1
  10.0 1.5 collective-permute-start
  11.7 4.5 %convolution_convert_fusion.1.refs_0_ = bf16[256,2048]{1,0:T(8,128)(2,1)} fusion(bf16[1024,2048]{1,0:T(8,128)(2,1)} %param.12, s32[256]{0:T(256)S(1)} %eq.68), kind=kOutput, calls=%fused_computation.3 | convolution fusion | flops 1074528256 | bytes 5243904 | tf_op jit(solution)/shard_map/dot_general | solution.py:296
  19.6 14.8 %shard_map.100.refs_6_ = f32[1664,512]{1,0:T(8,128)S(1)} custom-call(s32[16]{0:T(128)S(1)} %add.276.idx, bf16[512,2048]{1,0:T(8,128)(2,1)} %convolution_convert_fusion.refs_0_, bf16[512,2048]{1,0:T(8,128)(2,1)} %collective-permute-done.3.refs_1_, bf16[832,16384]{1,0:T(8,128)(2,1)} %refs_4_.5, bf16[832,16384]{1,0:T(8,128)(2,1)} %refs_5_.5, ...), custom_call_target="tpu_custom_call" | custom-call | flops 6979321856 | bytes 13631488 | tf_op jit(solution)/shard_map/pallas_call | solution.py:170
  34.4 10.7 %shard_map.101.refs_8_ = f32[1664,256]{1,0:T(8,128)S(1)} custom-call(s32[16]{0:T(128)S(1)} %add.276.idx, bf16[256,2048]{1,0:T(8,128)(2,1)} %convolution_convert_fusion.1.refs_0_, bf16[256,2048]{1,0:T(8,128)(2,1)S(1)} %collective-permute-done.2.refs_1_, bf16[832,16384]{1,0:T(8,128)(2,1)} %refs_4_.5, bf16[832,16384]{1,0:T(8,128)(2,1)} %refs_5_.5, ...), custom_call_target="tpu_custom_call" | custom-call | flops 3489660928 | bytes 13631488 | tf_op jit(solution)/shard_map/pallas_call | solution.py:170
  45.1 11.5 %collective-permute-done.1.refs_1_ = bf16[512,2048]{1,0:T(8,128)(2,1)} collective-permute-done((bf16[512,2048]{1,0:T(8,128)(2,1)}, bf16[512,2048]{1,0:T(8,128)(2,1)}, u32[]{:S(2)}, u32[]{:S(2)}) %collective-permute-start.1) | collective-permute-done | bytes 2097184 | tf_op jit(solution)/shard_map/ppermute | solution.py:25
  56.6 1.5 collective-permute-done.refs_0_
  58.6 1.3 slice.32
  59.9 1.3 slice.33
  61.2 1.6 collective-permute-start.5
  63.2 14.4 %shard_map.102.refs_6_ = f32[1664,512]{1,0:T(8,128)S(1)} custom-call(s32[16]{0:T(128)S(1)} %add.276.idx, bf16[512,2048]{1,0:T(8,128)(2,1)} %collective-permute-done.refs_0_, bf16[512,2048]{1,0:T(8,128)(2,1)} %collective-permute-done.1.refs_1_, bf16[832,16384]{1,0:T(8,128)(2,1)} %refs_4_.5, ...), custom_call_target="tpu_custom_call", output_to_operand_aliasing={{}: (7, {})} | custom-call | flops 6979321856 | bytes 13631488 | tf_op jit(solution)/shard_map/pallas_call | solution.py:170
  77.7 14.4 %shard_map.103.refs_8_ = f32[1664,512]{1,0:T(8,128)S(1)} custom-call(s32[16]{0:T(128)S(1)} %add.276.idx, bf16[512,2048]{1,0:T(8,128)(2,1)S(1)} %collective-permute-done.6.refs_0_, bf16[512,2048]{1,0:T(8,128)(2,1)S(1)} %collective-permute-done.7.refs_1_, bf16[832,16384]{1,0:T(8,128)(2,1)} %refs_4_.5, ...), custom_call_target="tpu_custom_call", output_to_operand_aliasing={{}: (7, {})} | custom-call | flops 6979321856 | bytes 13631488 | tf_op jit(solution)/shard_map/pallas_call | solution.py:170
  93.0 1.7 collective-permute-start.14
  94.8 1.5 collective-permute-done.9.refs_3_
  96.3 14.7 %shard_map.104 = bf16[512,896]{1,0:T(8,128)(2,1)S(1)} custom-call(s32[16]{0:T(128)S(1)} %add.276.idx, bf16[512,1024]{1,0:T(8,128)(2,1)S(1)} %collective-permute-done.4.refs_0_, bf16[512,1024]{1,0:T(8,128)(2,1)S(1)} %collective-permute-done.5.refs_1_, bf16[512,1024]{1,0:T(8,128)(2,1)S(1)} %collective-permute-done.8.refs_2_, ...), custom_call_target="tpu_custom_call" | custom-call | flops 6979321856 | bytes 13631488 | tf_op jit(solution)/shard_map/pallas_call | solution.py:170
  111.0 7.1 %collective-permute-done.13.refs_0_ = bf16[256,2048]{1,0:T(8,128)(2,1)} collective-permute-done((bf16[256,2048]{1,0:T(8,128)(2,1)}, bf16[256,2048]{1,0:T(8,128)(2,1)}, u32[]{:S(2)}, u32[]{:S(2)}) %collective-permute-start.13) | collective-permute-done | bytes 1048608 | tf_op jit(solution)/shard_map/ppermute | solution.py:25
  119.6 2.6 collective-permute-start.12
  125.4 4.0 %collective-permute-done.12 = bf16[128,896]{1,0:T(8,128)(2,1)} collective-permute-done((bf16[128,896]{1,0:T(8,128)(2,1)}, bf16[128,896]{1,0:T(8,128)(2,1)}, u32[]{:S(2)}, u32[]{:S(2)}) %collective-permute-start.12) | collective-permute-done | bytes 229408 | tf_op jit(solution)/shard_map/ppermute | solution.py:25
  129.3 1.7 collective-permute-start.23
  131.0 2.2 collective-permute-done.11
  133.2 1.7 collective-permute-start.22
  134.9 1.3 pad_maximum_fusion
  136.3 3.7 %collective-permute-start.17 = (bf16[128,896]{1,0:T(8,128)(2,1)S(1)}, bf16[128,896]{1,0:T(8,128)(2,1)S(1)}, u32[]{:S(2)}, u32[]{:S(2)}) collective-permute-start(bf16[128,896]{1,0:T(8,128)(2,1)S(1)} %get-tuple-element.100), channel_id=1, source_target_pairs={{0,3},{1,0},{2,1},{3,2},{4,7},{5,4},{6,5},{7,6},{8,11},{9,8},{10,9... | collective-permute-start | bytes 688136 | tf_op jit(solution)/shard_map/ppermute | solution.py:31
  141.0 18.1 %shard_map.105.refs_8_ = f32[1664,256]{1,0:T(8,128)S(1)} custom-call(s32[16]{0:T(128)S(1)} %add.276.idx, bf16[256,2048]{1,0:T(8,128)(2,1)} %collective-permute-done.13.refs_0_, bf16[256,2048]{1,0:T(8,128)(2,1)} %collective-permute-done.14.refs_1_, bf16[256,2048]{1,0:T(8,128)(2,1)} %collective-permute-done.18.refs_2_, ...), custom_call_target="tpu_custom_call", output_to_operand_aliasing={{}: (9, {})} | custom-call | flops 6979321856 | bytes 27262976 | tf_op jit(solution)/shard_map/pallas_call | solution.py:170
  159.2 1.2 copy-done.4
  164.4 1.5 collective-permute-start.20
  165.8 1.5 copy-done.5
  167.3 10.2 %shard_map.106 = bf16[256,896]{1,0:T(8,128)(2,1)S(1)} custom-call(s32[16]{0:T(128)S(1)} %add.276.idx, bf16[256,1024]{1,0:T(8,128)(2,1)S(1)} %collective-permute-done.22.refs_0_, bf16[256,1024]{1,0:T(8,128)(2,1)S(1)} %collective-permute-done.23.refs_1_, bf16[256,1024]{1,0:T(8,128)(2,1)} %collective-permute-done.24.refs_2_, ...), custom_call_target="tpu_custom_call" | custom-call | flops 3489660928 | bytes 13631488 | tf_op jit(solution)/shard_map/pallas_call | solution.py:170
  177.6 1.6 collective-permute-start.38
  179.7 1.5 collective-permute-start.36
  181.2 7.1 %collective-permute-done.21.refs_2_ = bf16[512,896]{1,0:T(8,128)(2,1)} collective-permute-done((bf16[512,896]{1,0:T(8,128)(2,1)}, bf16[512,896]{1,0:T(8,128)(2,1)}, u32[]{:S(2)}, u32[]{:S(2)}) %collective-permute-start.21) | collective-permute-done | bytes 917536 | tf_op jit(solution)/shard_map/ppermute | solution.py:25
  193.2 9.1 %collective-permute-done.27.refs_4_ = bf16[256,896]{1,0:T(8,128)(2,1)S(1)} collective-permute-done((bf16[256,896]{1,0:T(8,128)(2,1)S(1)}, bf16[256,896]{1,0:T(8,128)(2,1)S(1)}, u32[]{:S(2)}, u32[]{:S(2)}) %collective-permute-start.27) | collective-permute-done | bytes 458784 | tf_op jit(solution)/shard_map/ppermute | solution.py:25
  202.3 2.0 collective-permute-done.26.refs_3_
  205.5 2.9 collective-permute-start.41
  209.5 28.2 %shard_map.107 = bf16[512,2048]{1,0:T(8,128)(2,1)S(1)} custom-call(s32[8]{0:T(128)S(1)} %stack.74.idx, bf16[512,896]{1,0:T(8,128)(2,1)} %constant_dynamic-update-slice_fusion.refs_0_, bf16[512,896]{1,0:T(8,128)(2,1)} %collective-permute-done.20.refs_1_, bf16[512,896]{1,0:T(8,128)(2,1)} %collective-permute-done.21.refs_2_, ...), custom_call_target="tpu_custom_call" | custom-call | flops 13958643712 | bytes 27262976 | tf_op jit(solution)/shard_map/pallas_call | solution.py:237
  237.7 1.4 constant_dynamic-slice_fusion.8
  240.7 10.9 %collective-permute-done.43.refs_2_ = bf16[256,896]{1,0:T(8,128)(2,1)S(1)} collective-permute-done((bf16[256,896]{1,0:T(8,128)(2,1)S(1)}, bf16[256,896]{1,0:T(8,128)(2,1)S(1)}, u32[]{:S(2)}, u32[]{:S(2)}) %collective-permute-start.43) | collective-permute-done | bytes 458784 | tf_op jit(solution)/shard_map/ppermute | solution.py:25
  252.9 1.6 collective-permute-start.44
  255.0 3.7 %collective-permute-done.45.refs_4_ = bf16[128,896]{1,0:T(8,128)(2,1)S(1)} collective-permute-done((bf16[128,896]{1,0:T(8,128)(2,1)S(1)}, bf16[128,896]{1,0:T(8,128)(2,1)S(1)}, u32[]{:S(2)}, u32[]{:S(2)}) %collective-permute-start.45) | collective-permute-done | bytes 229408 | tf_op jit(solution)/shard_map/ppermute | solution.py:25
  259.2 3.3 collective-permute-start.35
  262.6 1.4 collective-permute-start.33
  264.0 18.0 %shard_map.108 = bf16[256,2048]{1,0:T(8,128)(2,1)S(1)} custom-call(s32[8]{0:T(128)S(1)} %stack.74.idx, bf16[256,896]{1,0:T(8,128)(2,1)S(1)} %constant_dynamic-update-slice_fusion.4.refs_0_, bf16[256,896]{1,0:T(8,128)(2,1)S(1)} %collective-permute-done.42.refs_1_, bf16[256,896]{1,0:T(8,128)(2,1)S(1)} %collective-permute-done.43.refs_2_, ...), custom_call_target="tpu_custom_call" | custom-call | flops 6979321856 | bytes 27262976 | tf_op jit(solution)/shard_map/pallas_call | solution.py:237
  282.1 2.5 collective-permute-start.53
  285.6 13.1 %collective-permute-start.51 = (bf16[64,2048]{1,0:T(8,128)(2,1)S(1)}, bf16[64,2048]{1,0:T(8,128)(2,1)S(1)}, u32[]{:S(2)}, u32[]{:S(2)}) collective-permute-start(bf16[64,2048]{1,0:T(8,128)(2,1)S(1)} %get-tuple-element.98), channel_id=1, source_target_pairs={{0,1},{1,2},{2,3},{3,0},{4,5},{5,6},{6,7},{7,4},{8,9},{9,10},{10,1... | collective-permute-start | bytes 786440 | tf_op jit(solution)/shard_map/ppermute | solution.py:31
  298.7 21.9 %collective-permute-done.34 = bf16[128,2048]{1,0:T(8,128)(2,1)} collective-permute-done((bf16[128,2048]{1,0:T(8,128)(2,1)}, bf16[128,2048]{1,0:T(8,128)(2,1)}, u32[]{:S(2)}, u32[]{:S(2)}) %collective-permute-start.34) | collective-permute-done | bytes 524320 | tf_op jit(solution)/shard_map/ppermute | solution.py:31
  320.7 10.7 %collective-permute-done.52 = bf16[64,2048]{1,0:T(8,128)(2,1)S(1)} collective-permute-done((bf16[64,2048]{1,0:T(8,128)(2,1)S(1)}, bf16[64,2048]{1,0:T(8,128)(2,1)S(1)}, u32[]{:S(2)}, u32[]{:S(2)}) %collective-permute-start.52) | collective-permute-done | bytes 262176 | tf_op jit(solution)/shard_map/ppermute | solution.py:31
  331.3 1.9 add_convert_fusion
  (150 shorter events, 30.9 us)
Async XLA Ops:
  7.0 12.6 %collective-permute-start.3 = (bf16[512,2048]{1,0:T(8,128)(2,1)}, bf16[512,2048]{1,0:T(8,128)(2,1)}, u32[]{:S(2)}, u32[]{:S(2)}) collective-permute-start(bf16[512,2048]{1,0:T(8,128)(2,1)} %convolution_convert_fusion.refs_0_), channel_id=1, source_target_pairs={{0,4},{4,0},{8,12},{12,8},{16,20},{20,16},{24,28},{28,24},{1,5},{5... | collective-permute-start | bytes 6291464 | tf_op jit(solution)/shard_map/ppermute | solution.py:25
  7.5 49.1 %collective-permute-start.1 = (bf16[512,2048]{1,0:T(8,128)(2,1)}, bf16[512,2048]{1,0:T(8,128)(2,1)}, u32[]{:S(2)}, u32[]{:S(2)}) collective-permute-start(bf16[512,2048]{1,0:T(8,128)(2,1)} %convolution_convert_fusion.refs_0_), channel_id=1, source_target_pairs={{0,16},{4,20},{8,24},{12,28},{16,0},{20,4},{24,8},{28,12},{1,17},{... | collective-permute-start | bytes 6291464 | tf_op jit(solution)/shard_map/ppermute | solution.py:25
  10.0 48.1 %collective-permute-start = (bf16[512,2048]{1,0:T(8,128)(2,1)}, bf16[512,2048]{1,0:T(8,128)(2,1)}, u32[]{:S(2)}, u32[]{:S(2)}) collective-permute-start(bf16[512,2048]{1,0:T(8,128)(2,1)} %convolution_convert_fusion.refs_0_), channel_id=1, source_target_pairs={{0,8},{4,12},{8,0},{12,4},{16,24},{20,28},{24,16},{28,20},{1,9},{5... | collective-permute-start | bytes 6291464 | tf_op jit(solution)/shard_map/ppermute | solution.py:25
  16.2 18.2 %collective-permute-start.2 = (bf16[256,2048]{1,0:T(8,128)(2,1)}, bf16[256,2048]{1,0:T(8,128)(2,1)S(1)}, u32[]{:S(2)}, u32[]{:S(2)}) collective-permute-start(bf16[256,2048]{1,0:T(8,128)(2,1)} %convolution_convert_fusion.1.refs_0_), channel_id=1, source_target_pairs={{0,4},{4,0},{8,12},{12,8},{16,20},{20,16},{24,28},{28,24},{1,5},{5... | collective-permute-start | bytes 3145736 | tf_op jit(solution)/shard_map/ppermute | solution.py:25
  58.1 19.6 %collective-permute-start.6 = (bf16[512,2048]{1,0:T(8,128)(2,1)}, bf16[512,2048]{1,0:T(8,128)(2,1)S(1)}, u32[]{:S(2)}, u32[]{:S(2)}) collective-permute-start(bf16[512,2048]{1,0:T(8,128)(2,1)} %collective-permute-done.refs_0_), channel_id=1, source_target_pairs={{0,4},{4,0},{8,12},{12,8},{16,20},{20,16},{24,28},{28,24},{1,5},{5... | collective-permute-start | bytes 6291464 | tf_op jit(solution)/shard_map/ppermute | solution.py:25
  58.1 19.6 %collective-permute-start.7 = (bf16[512,2048]{1,0:T(8,128)(2,1)}, bf16[512,2048]{1,0:T(8,128)(2,1)S(1)}, u32[]{:S(2)}, u32[]{:S(2)}) collective-permute-start(bf16[512,2048]{1,0:T(8,128)(2,1)} %collective-permute-done.1.refs_1_), channel_id=1, source_target_pairs={{0,4},{4,0},{8,12},{12,8},{16,20},{20,16},{24,28},{28,24},{1,5},{5... | collective-permute-start | bytes 6291464 | tf_op jit(solution)/shard_map/ppermute | solution.py:25
  61.2 30.9 %collective-permute-start.5 = (bf16[512,1024]{1,0:T(8,128)(2,1)S(1)}, bf16[512,1024]{1,0:T(8,128)(2,1)S(1)}, u32[]{:S(2)}, u32[]{:S(2)}) collective-permute-start(bf16[512,1024]{1,0:T(8,128)(2,1)S(1)} %slice.33), channel_id=1, source_target_pairs={{0,8},{4,12},{8,0},{12,4},{16,24},{20,28},{24,16},{28,20},{1,9},{5... | collective-permute-start | bytes 3145736 | tf_op jit(solution)/shard_map/ppermute | solution.py:25
  62.7 29.4 %collective-permute-start.4 = (bf16[512,1024]{1,0:T(8,128)(2,1)S(1)}, bf16[512,1024]{1,0:T(8,128)(2,1)S(1)}, u32[]{:S(2)}, u32[]{:S(2)}) collective-permute-start(bf16[512,1024]{1,0:T(8,128)(2,1)S(1)} %slice.32), channel_id=1, source_target_pairs={{0,16},{4,20},{8,24},{12,28},{16,0},{20,4},{24,8},{28,12},{1,17},{... | collective-permute-start | bytes 3145736 | tf_op jit(solution)/shard_map/ppermute | solution.py:25
  92.7 25.5 %collective-permute-start.13 = (bf16[256,2048]{1,0:T(8,128)(2,1)}, bf16[256,2048]{1,0:T(8,128)(2,1)}, u32[]{:S(2)}, u32[]{:S(2)}) collective-permute-start(bf16[256,2048]{1,0:T(8,128)(2,1)} %convolution_convert_fusion.1.refs_0_), channel_id=1, source_target_pairs={{0,8},{4,12},{8,0},{12,4},{16,24},{20,28},{24,16},{28,20},{1,9},{5... | collective-permute-start | bytes 3145736 | tf_op jit(solution)/shard_map/ppermute | solution.py:25
  93.0 25.2 %collective-permute-start.14 = (bf16[256,2048]{1,0:T(8,128)(2,1)}, bf16[256,2048]{1,0:T(8,128)(2,1)}, u32[]{:S(2)}, u32[]{:S(2)}) collective-permute-start(bf16[256,2048]{1,0:T(8,128)(2,1)} %convolution_convert_fusion.1.refs_0_), channel_id=1, source_target_pairs={{0,16},{4,20},{8,24},{12,28},{16,0},{20,4},{24,8},{28,12},{1,17},{... | collective-permute-start | bytes 3145736 | tf_op jit(solution)/shard_map/ppermute | solution.py:25
  118.2 21.8 %collective-permute-start.18 = (bf16[256,2048]{1,0:T(8,128)(2,1)}, bf16[256,2048]{1,0:T(8,128)(2,1)}, u32[]{:S(2)}, u32[]{:S(2)}) collective-permute-start(bf16[256,2048]{1,0:T(8,128)(2,1)} %collective-permute-done.13.refs_0_), channel_id=1, source_target_pairs={{0,4},{4,0},{8,12},{12,8},{16,20},{20,16},{24,28},{28,24},{1,5},{5... | collective-permute-start | bytes 3145736 | tf_op jit(solution)/shard_map/ppermute | solution.py:25
  118.2 21.8 %collective-permute-start.19 = (bf16[256,2048]{1,0:T(8,128)(2,1)}, bf16[256,2048]{1,0:T(8,128)(2,1)}, u32[]{:S(2)}, u32[]{:S(2)}) collective-permute-start(bf16[256,2048]{1,0:T(8,128)(2,1)} %collective-permute-done.14.refs_1_), channel_id=1, source_target_pairs={{0,4},{4,0},{8,12},{12,8},{16,20},{20,16},{24,28},{28,24},{1,5},{5... | collective-permute-start | bytes 3145736 | tf_op jit(solution)/shard_map/ppermute | solution.py:25
  119.6 9.7 %collective-permute-start.12 = (bf16[128,896]{1,0:T(8,128)(2,1)}, bf16[128,896]{1,0:T(8,128)(2,1)}, u32[]{:S(2)}, u32[]{:S(2)}) collective-permute-start(bf16[128,896]{1,0:T(8,128)(2,1)} %get-tuple-element.104), channel_id=1, source_target_pairs={{0,24},{4,28},{8,16},{12,20},{16,8},{20,12},{24,0},{28,4},{1,25},{... | collective-permute-start | bytes 688136 | tf_op jit(solution)/shard_map/ppermute | solution.py:25
  122.2 11.0 %collective-permute-start.11 = (bf16[128,896]{1,0:T(8,128)(2,1)}, bf16[128,896]{1,0:T(8,128)(2,1)}, u32[]{:S(2)}, u32[]{:S(2)}) collective-permute-start(bf16[128,896]{1,0:T(8,128)(2,1)} %get-tuple-element.105), channel_id=1, source_target_pairs={{0,16},{4,20},{8,24},{12,28},{16,0},{20,4},{24,8},{28,12},{1,17},{... | collective-permute-start | bytes 688136 | tf_op jit(solution)/shard_map/ppermute | solution.py:25
  122.7 12.2 %collective-permute-start.10 = (bf16[128,896]{1,0:T(8,128)(2,1)}, bf16[128,896]{1,0:T(8,128)(2,1)}, u32[]{:S(2)}, u32[]{:S(2)}) collective-permute-start(bf16[128,896]{1,0:T(8,128)(2,1)} %get-tuple-element.106), channel_id=1, source_target_pairs={{0,8},{4,12},{8,0},{12,4},{16,24},{20,28},{24,16},{28,20},{1,9},{5... | collective-permute-start | bytes 688136 | tf_op jit(solution)/shard_map/ppermute | solution.py:25
  129.3 31.1 %collective-permute-start.23 = (bf16[256,1024]{1,0:T(8,128)(2,1)S(1)}, bf16[256,1024]{1,0:T(8,128)(2,1)S(1)}, u32[]{:S(2)}, u32[]{:S(2)}) collective-permute-start(bf16[256,1024]{1,0:T(8,128)(2,1)S(1)} %slice.35), channel_id=1, source_target_pairs={{0,8},{4,12},{8,0},{12,4},{16,24},{20,28},{24,16},{28,20},{1,9},{5... | collective-permute-start | bytes 1572872 | tf_op jit(solution)/shard_map/ppermute | solution.py:25
  133.2 27.2 %collective-permute-start.22 = (bf16[256,1024]{1,0:T(8,128)(2,1)S(1)}, bf16[256,1024]{1,0:T(8,128)(2,1)S(1)}, u32[]{:S(2)}, u32[]{:S(2)}) collective-permute-start(bf16[256,1024]{1,0:T(8,128)(2,1)S(1)} %slice.34), channel_id=1, source_target_pairs={{0,16},{4,20},{8,24},{12,28},{16,0},{20,4},{24,8},{28,12},{1,17},{... | collective-permute-start | bytes 1572872 | tf_op jit(solution)/shard_map/ppermute | solution.py:25
  136.3 24.1 %collective-permute-start.17 = (bf16[128,896]{1,0:T(8,128)(2,1)S(1)}, bf16[128,896]{1,0:T(8,128)(2,1)S(1)}, u32[]{:S(2)}, u32[]{:S(2)}) collective-permute-start(bf16[128,896]{1,0:T(8,128)(2,1)S(1)} %get-tuple-element.100), channel_id=1, source_target_pairs={{0,3},{1,0},{2,1},{3,2},{4,7},{5,4},{6,5},{7,6},{8,11},{9,8},{10,9... | collective-permute-start | bytes 688136 | tf_op jit(solution)/shard_map/ppermute | solution.py:31
  140.0 20.4 %collective-permute-start.16 = (bf16[128,896]{1,0:T(8,128)(2,1)S(1)}, bf16[128,896]{1,0:T(8,128)(2,1)S(1)}, u32[]{:S(2)}, u32[]{:S(2)}) collective-permute-start(bf16[128,896]{1,0:T(8,128)(2,1)S(1)} %get-tuple-element.101), channel_id=1, source_target_pairs={{0,2},{1,3},{2,0},{3,1},{4,6},{5,7},{6,4},{7,5},{8,10},{9,11},{10,... | collective-permute-start | bytes 688136 | tf_op jit(solution)/shard_map/ppermute | solution.py:31
  140.0 20.4 %collective-permute-start.15 = (bf16[128,896]{1,0:T(8,128)(2,1)S(1)}, bf16[128,896]{1,0:T(8,128)(2,1)S(1)}, u32[]{:S(2)}, u32[]{:S(2)}) collective-permute-start(bf16[128,896]{1,0:T(8,128)(2,1)S(1)} %get-tuple-element.102), channel_id=1, source_target_pairs={{0,1},{1,2},{2,3},{3,0},{4,5},{5,6},{6,7},{7,4},{8,9},{9,10},{10,1... | collective-permute-start | bytes 688136 | tf_op jit(solution)/shard_map/ppermute | solution.py:31
  160.4 5.4 %collective-permute-start.24 = (bf16[256,1024]{1,0:T(8,128)(2,1)S(1)}, bf16[256,1024]{1,0:T(8,128)(2,1)}, u32[]{:S(2)}, u32[]{:S(2)}) collective-permute-start(bf16[256,1024]{1,0:T(8,128)(2,1)S(1)} %collective-permute-done.22.refs_0_), channel_id=1, source_target_pairs={{0,4},{4,0},{8,12},{12,8},{16,20},{20,16},{24,28},{28,24},{1,5},{5... | collective-permute-start | bytes 1572872 | tf_op jit(solution)/shard_map/ppermute | solution.py:25
  163.8 24.4 %collective-permute-start.21 = (bf16[512,896]{1,0:T(8,128)(2,1)}, bf16[512,896]{1,0:T(8,128)(2,1)}, u32[]{:S(2)}, u32[]{:S(2)}) collective-permute-start(bf16[512,896]{1,0:T(8,128)(2,1)} %constant_dynamic-update-slice_fusion.refs_0_), channel_id=1, source_target_pairs={{0,16},{4,20},{8,24},{12,28},{16,0},{20,4},{24,8},{28,12},{1,17},{... | collective-permute-start | bytes 2752520 | tf_op jit(solution)/shard_map/ppermute | solution.py:25
  164.4 23.9 %collective-permute-start.20 = (bf16[512,896]{1,0:T(8,128)(2,1)}, bf16[512,896]{1,0:T(8,128)(2,1)}, u32[]{:S(2)}, u32[]{:S(2)}) collective-permute-start(bf16[512,896]{1,0:T(8,128)(2,1)} %constant_dynamic-update-slice_fusion.refs_0_), channel_id=1, source_target_pairs={{0,8},{4,12},{8,0},{12,4},{16,24},{20,28},{24,16},{28,20},{1,9},{5... | collective-permute-start | bytes 2752520 | tf_op jit(solution)/shard_map/ppermute | solution.py:25
  177.6 14.0 %collective-permute-start.38 = (bf16[64,896]{1,0:T(8,128)(2,1)S(1)}, bf16[64,896]{1,0:T(8,128)(2,1)S(1)}, u32[]{:S(2)}, u32[]{:S(2)}) collective-permute-start(bf16[64,896]{1,0:T(8,128)(2,1)S(1)} %get-tuple-element.112), channel_id=1, source_target_pairs={{0,24},{4,28},{8,16},{12,20},{16,8},{20,12},{24,0},{28,4},{1,25},{... | collective-permute-start | bytes 344072 | tf_op jit(solution)/shard_map/ppermute | solution.py:25
  179.2 13.5 %collective-permute-start.37 = (bf16[64,896]{1,0:T(8,128)(2,1)S(1)}, bf16[64,896]{1,0:T(8,128)(2,1)}, u32[]{:S(2)}, u32[]{:S(2)}) collective-permute-start(bf16[64,896]{1,0:T(8,128)(2,1)S(1)} %get-tuple-element.113), channel_id=1, source_target_pairs={{0,16},{4,20},{8,24},{12,28},{16,0},{20,4},{24,8},{28,12},{1,17},{... | collective-permute-start | bytes 344072 | tf_op jit(solution)/shard_map/ppermute | solution.py:25
  179.7 13.0 %collective-permute-start.36 = (bf16[64,896]{1,0:T(8,128)(2,1)S(1)}, bf16[64,896]{1,0:T(8,128)(2,1)}, u32[]{:S(2)}, u32[]{:S(2)}) collective-permute-start(bf16[64,896]{1,0:T(8,128)(2,1)S(1)} %get-tuple-element.114), channel_id=1, source_target_pairs={{0,8},{4,12},{8,0},{12,4},{16,24},{20,28},{24,16},{28,20},{1,9},{5... | collective-permute-start | bytes 344072 | tf_op jit(solution)/shard_map/ppermute | solution.py:25
  188.2 17.2 %collective-permute-start.28 = (bf16[512,896]{1,0:T(8,128)(2,1)}, bf16[512,896]{1,0:T(8,128)(2,1)S(1)}, u32[]{:S(2)}, u32[]{:S(2)}) collective-permute-start(bf16[512,896]{1,0:T(8,128)(2,1)} %constant_dynamic-update-slice_fusion.refs_0_), channel_id=1, source_target_pairs={{0,4},{4,0},{8,12},{12,8},{16,20},{20,16},{24,28},{28,24},{1,5},{5... | collective-permute-start | bytes 2752520 | tf_op jit(solution)/shard_map/ppermute | solution.py:25
  189.3 13.0 %collective-permute-start.27 = (bf16[256,896]{1,0:T(8,128)(2,1)S(1)}, bf16[256,896]{1,0:T(8,128)(2,1)S(1)}, u32[]{:S(2)}, u32[]{:S(2)}) collective-permute-start(bf16[256,896]{1,0:T(8,128)(2,1)S(1)} %slice.37), channel_id=1, source_target_pairs={{0,8},{4,12},{8,0},{12,4},{16,24},{20,28},{24,16},{28,20},{1,9},{5... | collective-permute-start | bytes 1376264 | tf_op jit(solution)/shard_map/ppermute | solution.py:25
  191.6 12.7 %collective-permute-start.26 = (bf16[256,896]{1,0:T(8,128)(2,1)S(1)}, bf16[256,896]{1,0:T(8,128)(2,1)}, u32[]{:S(2)}, u32[]{:S(2)}) collective-permute-start(bf16[256,896]{1,0:T(8,128)(2,1)S(1)} %slice.36), channel_id=1, source_target_pairs={{0,16},{4,20},{8,24},{12,28},{16,0},{20,4},{24,8},{28,12},{1,17},{... | collective-permute-start | bytes 1376264 | tf_op jit(solution)/shard_map/ppermute | solution.py:25
  192.7 16.8 %collective-permute-start.29 = (bf16[512,896]{1,0:T(8,128)(2,1)}, bf16[512,896]{1,0:T(8,128)(2,1)S(1)}, u32[]{:S(2)}, u32[]{:S(2)}) collective-permute-start(bf16[512,896]{1,0:T(8,128)(2,1)} %collective-permute-done.20.refs_1_), channel_id=1, source_target_pairs={{0,4},{4,0},{8,12},{12,8},{16,20},{20,16},{24,28},{28,24},{1,5},{5... | collective-permute-start | bytes 2752520 | tf_op jit(solution)/shard_map/ppermute | solution.py:25
  192.7 16.8 %collective-permute-start.30 = (bf16[512,896]{1,0:T(8,128)(2,1)}, bf16[512,896]{1,0:T(8,128)(2,1)S(1)}, u32[]{:S(2)}, u32[]{:S(2)}) collective-permute-start(bf16[512,896]{1,0:T(8,128)(2,1)} %collective-permute-done.21.refs_2_), channel_id=1, source_target_pairs={{0,4},{4,0},{8,12},{12,8},{16,20},{20,16},{24,28},{28,24},{1,5},{5... | collective-permute-start | bytes 2752520 | tf_op jit(solution)/shard_map/ppermute | solution.py:25
  202.3 6.1 %collective-permute-start.32 = (bf16[256,896]{1,0:T(8,128)(2,1)S(1)}, bf16[256,896]{1,0:T(8,128)(2,1)}, u32[]{:S(2)}, u32[]{:S(2)}) collective-permute-start(bf16[256,896]{1,0:T(8,128)(2,1)S(1)} %collective-permute-done.27.refs_4_), channel_id=1, source_target_pairs={{0,4},{4,0},{8,12},{12,8},{16,20},{20,16},{24,28},{28,24},{1,5},{5... | collective-permute-start | bytes 1376264 | tf_op jit(solution)/shard_map/ppermute | solution.py:25
  205.5 33.6 %collective-permute-start.41 = (bf16[64,896]{1,0:T(8,128)(2,1)S(1)}, bf16[64,896]{1,0:T(8,128)(2,1)S(1)}, u32[]{:S(2)}, u32[]{:S(2)}) collective-permute-start(bf16[64,896]{1,0:T(8,128)(2,1)S(1)} %get-tuple-element.108), channel_id=1, source_target_pairs={{0,3},{1,0},{2,1},{3,2},{4,7},{5,4},{6,5},{7,6},{8,11},{9,8},{10,9... | collective-permute-start | bytes 344072 | tf_op jit(solution)/shard_map/ppermute | solution.py:31
  208.4 30.7 %collective-permute-start.40 = (bf16[64,896]{1,0:T(8,128)(2,1)S(1)}, bf16[64,896]{1,0:T(8,128)(2,1)S(1)}, u32[]{:S(2)}, u32[]{:S(2)}) collective-permute-start(bf16[64,896]{1,0:T(8,128)(2,1)S(1)} %get-tuple-element.109), channel_id=1, source_target_pairs={{0,2},{1,3},{2,0},{3,1},{4,6},{5,7},{6,4},{7,5},{8,10},{9,11},{10,... | collective-permute-start | bytes 344072 | tf_op jit(solution)/shard_map/ppermute | solution.py:31
  209.5 29.6 %collective-permute-start.39 = (bf16[64,896]{1,0:T(8,128)(2,1)S(1)}, bf16[64,896]{1,0:T(8,128)(2,1)S(1)}, u32[]{:S(2)}, u32[]{:S(2)}) collective-permute-start(bf16[64,896]{1,0:T(8,128)(2,1)S(1)} %get-tuple-element.110), channel_id=1, source_target_pairs={{0,1},{1,2},{2,3},{3,0},{4,5},{5,6},{6,7},{7,4},{8,9},{9,10},{10,1... | collective-permute-start | bytes 344072 | tf_op jit(solution)/shard_map/ppermute | solution.py:31
  239.2 12.4 %collective-permute-start.43 = (bf16[256,896]{1,0:T(8,128)(2,1)S(1)}, bf16[256,896]{1,0:T(8,128)(2,1)S(1)}, u32[]{:S(2)}, u32[]{:S(2)}) collective-permute-start(bf16[256,896]{1,0:T(8,128)(2,1)S(1)} %constant_dynamic-update-slice_fusion.4.refs_0_), channel_id=1, source_target_pairs={{0,16},{4,20},{8,24},{12,28},{16,0},{20,4},{24,8},{28,12},{1,17},{... | collective-permute-start | bytes 1376264 | tf_op jit(solution)/shard_map/ppermute | solution.py:25
  240.2 12.1 %collective-permute-start.42 = (bf16[256,896]{1,0:T(8,128)(2,1)S(1)}, bf16[256,896]{1,0:T(8,128)(2,1)S(1)}, u32[]{:S(2)}, u32[]{:S(2)}) collective-permute-start(bf16[256,896]{1,0:T(8,128)(2,1)S(1)} %constant_dynamic-update-slice_fusion.4.refs_0_), channel_id=1, source_target_pairs={{0,8},{4,12},{8,0},{12,4},{16,24},{20,28},{24,16},{28,20},{1,9},{5... | collective-permute-start | bytes 1376264 | tf_op jit(solution)/shard_map/ppermute | solution.py:25
  240.7 18.5 %collective-permute-start.46 = (bf16[256,896]{1,0:T(8,128)(2,1)S(1)}, bf16[256,896]{1,0:T(8,128)(2,1)S(1)}, u32[]{:S(2)}, u32[]{:S(2)}) collective-permute-start(bf16[256,896]{1,0:T(8,128)(2,1)S(1)} %constant_dynamic-update-slice_fusion.4.refs_0_), channel_id=1, source_target_pairs={{0,4},{4,0},{8,12},{12,8},{16,20},{20,16},{24,28},{28,24},{1,5},{5... | collective-permute-start | bytes 1376264 | tf_op jit(solution)/shard_map/ppermute | solution.py:25
  252.3 6.4 %collective-permute-start.45 = (bf16[128,896]{1,0:T(8,128)(2,1)S(1)}, bf16[128,896]{1,0:T(8,128)(2,1)S(1)}, u32[]{:S(2)}, u32[]{:S(2)}) collective-permute-start(bf16[128,896]{1,0:T(8,128)(2,1)S(1)} %slice.39), channel_id=1, source_target_pairs={{0,8},{4,12},{8,0},{12,4},{16,24},{20,28},{24,16},{28,20},{1,9},{5... | collective-permute-start | bytes 688136 | tf_op jit(solution)/shard_map/ppermute | solution.py:25
  252.9 6.2 %collective-permute-start.44 = (bf16[128,896]{1,0:T(8,128)(2,1)S(1)}, bf16[128,896]{1,0:T(8,128)(2,1)S(1)}, u32[]{:S(2)}, u32[]{:S(2)}) collective-permute-start(bf16[128,896]{1,0:T(8,128)(2,1)S(1)} %slice.38), channel_id=1, source_target_pairs={{0,16},{4,20},{8,24},{12,28},{16,0},{20,4},{24,8},{28,12},{1,17},{... | collective-permute-start | bytes 688136 | tf_op jit(solution)/shard_map/ppermute | solution.py:25
  254.5 9.5 %collective-permute-start.47 = (bf16[256,896]{1,0:T(8,128)(2,1)S(1)}, bf16[256,896]{1,0:T(8,128)(2,1)S(1)}, u32[]{:S(2)}, u32[]{:S(2)}) collective-permute-start(bf16[256,896]{1,0:T(8,128)(2,1)S(1)} %collective-permute-done.42.refs_1_), channel_id=1, source_target_pairs={{0,4},{4,0},{8,12},{12,8},{16,20},{20,16},{24,28},{28,24},{1,5},{5... | collective-permute-start | bytes 1376264 | tf_op jit(solution)/shard_map/ppermute | solution.py:25
  254.5 9.5 %collective-permute-start.48 = (bf16[256,896]{1,0:T(8,128)(2,1)S(1)}, bf16[256,896]{1,0:T(8,128)(2,1)S(1)}, u32[]{:S(2)}, u32[]{:S(2)}) collective-permute-start(bf16[256,896]{1,0:T(8,128)(2,1)S(1)} %collective-permute-done.43.refs_2_), channel_id=1, source_target_pairs={{0,4},{4,0},{8,12},{12,8},{16,20},{20,16},{24,28},{28,24},{1,5},{5... | collective-permute-start | bytes 1376264 | tf_op jit(solution)/shard_map/ppermute | solution.py:25
  259.2 26.4 %collective-permute-start.35 = (bf16[128,2048]{1,0:T(8,128)(2,1)}, bf16[128,2048]{1,0:T(8,128)(2,1)}, u32[]{:S(2)}, u32[]{:S(2)}) collective-permute-start(bf16[128,2048]{1,0:T(8,128)(2,1)} %get-tuple-element.92), channel_id=1, source_target_pairs={{0,3},{1,0},{2,1},{3,2},{4,7},{5,4},{6,5},{7,6},{8,11},{9,8},{10,9... | collective-permute-start | bytes 1572872 | tf_op jit(solution)/shard_map/ppermute | solution.py:31
  262.5 58.1 %collective-permute-start.34 = (bf16[128,2048]{1,0:T(8,128)(2,1)}, bf16[128,2048]{1,0:T(8,128)(2,1)}, u32[]{:S(2)}, u32[]{:S(2)}) collective-permute-start(bf16[128,2048]{1,0:T(8,128)(2,1)} %get-tuple-element.93), channel_id=1, source_target_pairs={{0,2},{1,3},{2,0},{3,1},{4,6},{5,7},{6,4},{7,5},{8,10},{9,11},{10,... | collective-permute-start | bytes 1572872 | tf_op jit(solution)/shard_map/ppermute | solution.py:31
  262.6 58.1 %collective-permute-start.33 = (bf16[128,2048]{1,0:T(8,128)(2,1)}, bf16[128,2048]{1,0:T(8,128)(2,1)}, u32[]{:S(2)}, u32[]{:S(2)}) collective-permute-start(bf16[128,2048]{1,0:T(8,128)(2,1)} %get-tuple-element.94), channel_id=1, source_target_pairs={{0,1},{1,2},{2,3},{3,0},{4,5},{5,6},{6,7},{7,4},{8,9},{9,10},{10,1... | collective-permute-start | bytes 1572872 | tf_op jit(solution)/shard_map/ppermute | solution.py:31
  282.1 38.6 %collective-permute-start.53 = (bf16[64,2048]{1,0:T(8,128)(2,1)S(1)}, bf16[64,2048]{1,0:T(8,128)(2,1)S(1)}, u32[]{:S(2)}, u32[]{:S(2)}) collective-permute-start(bf16[64,2048]{1,0:T(8,128)(2,1)S(1)} %get-tuple-element.96), channel_id=1, source_target_pairs={{0,3},{1,0},{2,1},{3,2},{4,7},{5,4},{6,5},{7,6},{8,11},{9,8},{10,9... | collective-permute-start | bytes 786440 | tf_op jit(solution)/shard_map/ppermute | solution.py:31
  284.6 46.8 %collective-permute-start.52 = (bf16[64,2048]{1,0:T(8,128)(2,1)S(1)}, bf16[64,2048]{1,0:T(8,128)(2,1)S(1)}, u32[]{:S(2)}, u32[]{:S(2)}) collective-permute-start(bf16[64,2048]{1,0:T(8,128)(2,1)S(1)} %get-tuple-element.97), channel_id=1, source_target_pairs={{0,2},{1,3},{2,0},{3,1},{4,6},{5,7},{6,4},{7,5},{8,10},{9,11},{10,... | collective-permute-start | bytes 786440 | tf_op jit(solution)/shard_map/ppermute | solution.py:31
  285.6 45.7 %collective-permute-start.51 = (bf16[64,2048]{1,0:T(8,128)(2,1)S(1)}, bf16[64,2048]{1,0:T(8,128)(2,1)S(1)}, u32[]{:S(2)}, u32[]{:S(2)}) collective-permute-start(bf16[64,2048]{1,0:T(8,128)(2,1)S(1)} %get-tuple-element.98), channel_id=1, source_target_pairs={{0,1},{1,2},{2,3},{3,0},{4,5},{5,6},{6,7},{7,4},{8,9},{9,10},{10,1... | collective-permute-start | bytes 786440 | tf_op jit(solution)/shard_map/ppermute | solution.py:31
  (15 other events, 175.4 us)

commit v2 on v1

--- a/solution.py
+++ b/solution.py
@@ -68,7 +68,7 @@
 
     for r in level:
         if r.bit_count() == 1:
-            got[r] = [swap(got[0][0], r)]
+            got[r] = [swap(p, r) for p in got[0]]
         else:
             got[r] = [swap(part(got[r ^ d], i), d) for i, d in enumerate(last_flips(r))]
 
@@ -289,35 +289,50 @@
     by_owner = by_owner.reshape(n_tp, share)
     requests = jnp.arange(pool.shape[0], dtype=jnp.int32)
 
-    def pick(begin, end):
+    def pick(begin, end, n_pieces):
         rr = (end - begin) // members
         named = by_owner[:, begin:end].reshape(n_tp, members, rr).transpose(1, 0, 2)
         chosen = (named.reshape(-1, 1) == requests).astype(jnp.bfloat16)
-        picked = jnp.dot(chosen, pool, preferred_element_type=jnp.float32)
-        return picked.astype(jnp.bfloat16)
-
-    halves = jnp.arange(HALVES, dtype=jnp.int32)
-
-    def columns_of(masks_in_order):
-        flipped = f ^ jnp.array(masks_in_order, dtype=jnp.int32)
-        return (flipped[:, None] * HALVES + halves).reshape(-1)
-
-    visits = [0, 1]
-    for c in range(2):
-        visits += [r ^ c for r in near[0]]
-    for c in range(2):
-        visits += [r ^ c for level in near[1:] for r in level]
-    columns = columns_of(visits)
-
-    def gate_up_part(wanted, acc, last):
+        size = width // n_pieces
+        return [
+            jnp.dot(
+                chosen,
+                pool[:, i * size : (i + 1) * size],
+                preferred_element_type=jnp.float32,
+            ).astype(jnp.bfloat16)
+            for i in range(n_pieces)
+        ]
+
+    far = [r for level in near[1:] for r in level]
+    visits = [(c, h) for c in range(2) for h in range(HALVES)]
+    visits += [(r ^ c, h) for h in range(HALVES) for c in range(2) for r in near[0]]
+    visits += [(r ^ c, h) for c in range(2) for r in far for h in range(HALVES)]
+    flipped = f ^ jnp.array([r for r, _ in visits], dtype=jnp.int32)
+    columns = flipped * HALVES + jnp.array([h for _, h in visits], dtype=jnp.int32)
+
+    def wanted(got, core_flip, group, halves=range(HALVES)):
+        found = []
+        for r in group:
+            for h in halves:
+                pieces = got[r]
+                if len(pieces) > 1:
+                    found.append((r ^ core_flip, h, pieces[h], 0))
+                else:
+                    found.append((r ^ core_flip, h, pieces[0], h))
+        return found
+
+    def hold_all(found, *others):
+        held = after([a for _, _, a, _ in found], *others)
+        return [(r, h, a, j) for (r, h, _, j), a in zip(found, held)]
+
+    def gate_up_part(found, acc, last):
+        found = sorted(found, key=lambda w: visits.index(w[:2]))
         arrays, parts = [], []
-        for r, c, pieces in wanted:
-            for p in pieces:
-                for j in range(HALVES // len(pieces)):
-                    parts.append((len(arrays), j))
-                arrays.append(p)
-        r, c, _ = wanted[0]
-        at = visits.index(r ^ c) * HALVES
+        for _, _, a, j in found:
+            if not any(a is b for b in arrays):
+                arrays.append(a)
+            parts.append(([a is b for b in arrays].index(True), j))
+        at = visits.index(found[0][:2])
         return gate_up(
             width // HALVES, arrays, tuple(parts), at, columns, weights, acc, last
         )
@@ -385,10 +400,8 @@
 
     n = len(CHUNKS)
     ends = [share * sum(CHUNKS[: i + 1]) // sum(CHUNKS) for i in range(n)]
-    own = [pick(b, e) for b, e in zip([0] + ends[:-1], ends)]
-    tokens = [{0: [x]} for x in own]
-
-    far = [r for level in near[1:] for r in level]
+    first = {0: pick(0, ends[0], HALVES)}
+    last = {0: pick(ends[0], ends[1], 1)}
 
     def blocks_of(got, group):
         return [got[r] for r in group]
@@ -409,62 +422,64 @@
     def twins_of(got, group):
         return {r: other_core(got[r]) for r in group}
 
-    def hold_all(pieces, *others):
-        held = after([p for _, _, p in pieces], *others)
-        return [(r, c, p) for (r, c, _), p in zip(pieces, held)]
-
-    def wanted(got, core_flip, group):
-        return [(r, core_flip, got[r]) for r in group]
-
-    first, last = tokens
-
-    spread(first, near[0], 1)
-    here = [wanted(x, 0, [0]) + wanted(twins_of(x, [0]), 1, [0]) for x in tokens]
-    acc_first = gate_up_part(here[0], None, False)
-    acc_last = gate_up_part(hold_all(here[1], acc_first), None, False)
-
-    hold(first, near[0], acc_last)
+    sent = []
+    for h in range(HALVES):
+        sent.append([swap(first[0][h], r) for r in near[0]])
+    acc_first = gate_up_part(
+        wanted(first, 0, [0]) + wanted(twins_of(first, [0]), 1, [0]), None, False
+    )
+    sent[0] = after(sent[0], acc_first)
+    twins = {r: [swap(p, 1)] for r, p in zip(near[0], sent[0])}
+    acc_last = wanted(last, 0, [0]) + wanted(twins_of(last, [0]), 1, [0])
+    acc_last = gate_up_part(hold_all(acc_last, acc_first, sent[0]), None, False)
+    pieces = [(r, 0, p, 0) for r, p in zip(near[0], sent[0])]
+    pieces += [(r ^ 1, 0, twins[r][0], 0) for r in near[0]]
+    acc_first = gate_up_part(hold_all(pieces, acc_last), acc_first, False)
+    for h in range(1, HALVES):
+        sent[h] = after(sent[h], acc_first)
+    for i, r in enumerate(near[0]):
+        first[r] = [sent[h][i] for h in range(HALVES)]
     far_blocks(first, 1)
-    twins = twins_of(first, near[0])
-    last[0] = after(last[0], blocks_of(first, near[0]))
+    last[0] = after(last[0], sent[1:])
     spread(last, near[0], 1)
-    acc_first = gate_up_part(wanted(first, 0, near[0]), acc_first, False)
-    acc_first = gate_up_part(wanted(twins, 1, near[0]), acc_first, False)
+    for h in range(1, HALVES):
+        pieces = [(r, h, p, 0) for r, p in zip(near[0], sent[h])]
+        pieces += [(r ^ 1, h, swap(p, 1), 0) for r, p in zip(near[0], sent[h])]
+        acc_first = gate_up_part(pieces, acc_first, False)
     hold(first, far, acc_first)
     pieces = wanted(first, 0, far) + wanted(twins_of(first, far), 1, far)
     hidden_first = gate_up_part(pieces, acc_first, True)
     moved_first = scatter(hidden_first)
 
-    hold(last, near[0], hidden_first)
+    hold(last, near[0], moved_first)
+    moved_first = to_planes(moved_first)
     far_blocks(last, 1)
     twins = twins_of(last, near[0])
-    moved_first = to_planes(after(moved_first, blocks_of(last, near[0])))
     pieces = wanted(last, 0, near[0]) + wanted(twins, 1, near[0])
     acc_last = gate_up_part(hold_all(pieces, moved_first[0]), acc_last, False)
     hold(last, far, acc_last)
+    landed_first = land(after(moved_first, acc_last))
     twins = twins_of(last, far)
-    landed_first = land(after(moved_first, acc_last))
     pieces = wanted(last, 0, far) + wanted(twins, 1, far)
     hidden_last = gate_up_part(pieces, acc_last, True)
     moved_last = scatter(hidden_last)
 
-    hold(landed_first, near[0], hidden_last)
+    hold(landed_first, near[0], moved_last[0])
     far_blocks(landed_first, 0)
     twins = twins_of(landed_first, [0] + near[0])
-    moved_last = to_planes(after(moved_last, blocks_of(landed_first, near[0])))
+    moved_last = to_planes(moved_last)
     twins.update(twins_of(landed_first, far))
-    partial_first = down_part((landed_first, twins))
+    partial_first = down_part(after((landed_first, twins), moved_last[0]))
     shares_first = exchange(partial_first)
     landed_last = land(after(moved_last, shares_first[0]))
 
-    hold(landed_last, near[0], partial_first)
+    hold(landed_last, near[0], shares_first[0])
     far_blocks(landed_last, 0)
     twins = twins_of(landed_last, masks)
-    partial_last = down_part((landed_last, twins))
-    shares_last = exchange(partial_last)
+    shares_last = exchange(down_part((landed_last, twins)))
     shares_first, shares_last = after((shares_first, shares_last))
-    mixed = [total(shares_first), total(shares_last)]
-    return jnp.concatenate(mixed).reshape(steps, share // steps, width)
+    mixed = jnp.concatenate([total(shares_first), total(shares_last)])
+    return mixed.reshape(steps, share // steps, width)
 
 
 def solution(mesh):

time: 335 us -> 325 us (0.970)
  starting transfers between devices: 60.5 us -> 49.8 us
    ppermute x12, starting transfers between devices: 30.1 us -> 17.9 us  [shift(): lax.ppermute(rows_first(block), 'tp', [(i, (i + by) % n) for i in range(n)])]
    ppermute x42 -> x47, waiting for transfers between devices: 61.8 us -> 54.2 us  [swap(): lax.ppermute(rows_first(block), 'fsdp', [(i, i ^ mask) for i in range(n)])]
    ppermute x12, waiting for transfers between devices: 32.6 us -> 39.9 us  [shift(): lax.ppermute(rows_first(block), 'tp', [(i, (i + by) % n) for i in range(n)])]
    unnamed x35 -> x57, local copies, waits for them, and re-layouts: 7.25 us -> 11.7 us
    slice x8 -> x6, local copies, waits for them, and re-layouts: 7.02 us -> 3.33 us  [part(): return lax.slice_in_dim(pieces[0], i * size, (i + 1) * size, axis=axis)]
    ppermute x42 -> x47, starting transfers between devices: 30.4 us -> 32 us  [swap(): lax.ppermute(rows_first(block), 'fsdp', [(i, i ^ mask) for i in range(n)])]
    dot_general x2 -> x3, matrix products: 10.4 us -> 10.8 us  [pick(): jnp.dot(chosen, pool[:, i * size:(i + 1) * size], preferred_element_type=...]
  transfers between devices with their start and end apart: 54 -> 59, of which waited for: 17 -> 21; matrix products, arithmetic and copies ran while one was open for 7% -> 6% of each run, Pallas kernels for 43% -> 44%
where the time goes in v2:
time: 325 us; the launch traced here: 322 us
  Pallas kernels  142 us (44%)
  waiting for transfers between devices  94.1 us (29%)
  starting transfers between devices  49.8 us (15%)
  local copies, waits for them, and re-layouts  20.5 us (6%)
  matrix products  10.8 us (3%)
    pallas_call x7, Pallas kernels, gate_up(): pl.pallas_call(functools.partial(gate_up_kernel, parts, acc is None, last...  97.4 us
    ppermute x47, waiting for transfers between devices, swap(): lax.ppermute(rows_first(block), 'fsdp', [(i, i ^ mask) for i in range(n)])  54.2 us
    pallas_call x2, Pallas kernels, down(): pl.pallas_call(functools.partial(down_kernel, sources, n_tp), grid_spec=p...  45.1 us
    ppermute x12, waiting for transfers between devices, shift(): lax.ppermute(rows_first(block), 'tp', [(i, (i + by) % n) for i in range(n)])  39.9 us
    ppermute x47, starting transfers between devices, swap(): lax.ppermute(rows_first(block), 'fsdp', [(i, i ^ mask) for i in range(n)])  32 us
    ppermute x12, starting transfers between devices, shift(): lax.ppermute(rows_first(block), 'tp', [(i, (i + by) % n) for i in range(n)])  17.9 us
    unnamed x57, local copies, waits for them, and re-layouts  11.7 us
    dot_general x3, matrix products, pick(): jnp.dot(chosen, pool[:, i * size:(i + 1) * size], preferred_element_type=...  10.8 us
  transfers between devices with their start and end apart: 59, of which 21 were waited for; matrix products, arithmetic and copies ran while one was open for 6% of the time, Pallas kernels for 44%

profile of v2, /device:TPU:0, one launch (start us, length us, event | category | flops | bytes accessed | tf_op | source)
XLA Modules:
  0.0 321.5 jit_solution(9907050336648841892)
XLA Ops:
  1.1 4.0 %fusion.4.refs_0_ = bf16[512,1024]{1,0:T(8,128)(2,1)} fusion(bf16[1024,2048]{1,0:T(8,128)(2,1)} %param.13, s32[512]{0:T(512)S(1)} %eq.64), kind=kOutput, calls=%fused_computation.8 | convolution fusion | flops 1074790400 | bytes 3147776 | tf_op jit(solution)/shard_map/dot_general | solution.py:298
  5.6 2.5 collective-permute-start
  8.1 1.5 collective-permute-start.1
  9.6 2.3 fusion.7.refs_1_
  12.1 4.5 %convolution_convert_fusion.refs_0_.refs_1_ = bf16[256,2048]{1,0:T(8,128)(2,1)} fusion(bf16[1024,2048]{1,0:T(8,128)(2,1)} %param.13, s32[256]{0:T(256)S(1)} %eq.68), kind=kOutput, calls=%fused_computation.2 | convolution fusion | flops 1074528256 | bytes 5243904 | tf_op jit(solution)/shard_map/dot_general | solution.py:298
  20.5 14.6 %shard_map.109.refs_8_ = f32[1664,512]{1,0:T(8,128)S(1)} custom-call(s32[16]{0:T(128)S(1)} %multiply_add_fusion.idx, bf16[512,1024]{1,0:T(8,128)(2,1)} %fusion.4.refs_0_, bf16[512,1024]{1,0:T(8,128)(2,1)} %fusion.7.refs_1_, bf16[512,1024]{1,0:T(8,128)(2,1)} %collective-permute-done.2.refs_2_, bf16[512,1024]{1,0:T(8,128)(2,1)} %collective-permute-done.3.refs_3_, ...), custom_call_target="tpu_custom_call" | custom-call | flops 6979321856 | bytes 13631488 | tf_op jit(solution)/shard_map/pallas_call | solution.py:170
  36.2 10.7 %shard_map.110.refs_12_ = f32[1664,256]{1,0:T(8,128)S(1)} custom-call(s32[16]{0:T(128)S(1)} %multiply_add_fusion.idx, bf16[256,2048]{1,0:T(8,128)(2,1)} %convolution_convert_fusion.refs_0_.refs_1_, bf16[256,2048]{1,0:T(8,128)(2,1)} %convolution_convert_fusion.refs_0_.refs_1_, bf16[256,2048]{1,0:T(8,128)(2,1)S(1)} %collective-permute-done.9.refs_2_.refs_3_, ...), custom_call_target="tpu_custom_call" | custom-call | flops 3489660928 | bytes 13631488 | tf_op jit(solution)/shard_map/pallas_call | solution.py:170
  47.0 14.6 %shard_map.111.refs_8_ = f32[1664,512]{1,0:T(8,128)S(1)} custom-call(s32[16]{0:T(128)S(1)} %multiply_add_fusion.idx, bf16[512,1024]{1,0:T(8,128)(2,1)} %collective-permute-done.refs_0_, bf16[512,1024]{1,0:T(8,128)(2,1)} %collective-permute-done.1.refs_1_, bf16[512,1024]{1,0:T(8,128)(2,1)S(1)} %collective-permute-done.7.refs_2_, ...), custom_call_target="tpu_custom_call", output_to_operand_aliasing={{}: (9, {})} | custom-call | flops 6979321856 | bytes 13631488 | tf_op jit(solution)/shard_map/pallas_call | solution.py:170
  62.2 2.0 collective-permute-start.4
  64.2 1.5 collective-permute-start.10
  65.8 13.9 %shard_map.112.refs_8_ = f32[1664,512]{1,0:T(8,128)S(1)} custom-call(s32[16]{0:T(128)S(1)} %multiply_add_fusion.idx, bf16[512,1024]{1,0:T(8,128)(2,1)S(1)} %collective-permute-done.5.refs_0_, bf16[512,1024]{1,0:T(8,128)(2,1)S(1)} %collective-permute-done.6.refs_1_, ...), custom_call_target="tpu_custom_call", output_to_operand_aliasing={{}: (9, {})} | custom-call | flops 6979321856 | bytes 13631488 | tf_op jit(solution)/shard_map/pallas_call | solution.py:170
  79.7 1.7 copy-done.2
  81.5 6.4 %collective-permute-done.4.refs_0_ = bf16[512,1024]{1,0:T(8,128)(2,1)} collective-permute-done((bf16[512,1024]{1,0:T(8,128)(2,1)}, bf16[512,1024]{1,0:T(8,128)(2,1)}, u32[]{:S(2)}, u32[]{:S(2)}) %collective-permute-start.4) | collective-permute-done | bytes 1048608 | tf_op jit(solution)/shard_map/ppermute | solution.py:25
  89.7 1.5 collective-permute-start.21
  92.1 1.5 collective-permute-done.14.refs_3_
  93.6 2.0 copy-done.3
  95.6 15.2 %shard_map.113 = bf16[512,896]{1,0:T(8,128)(2,1)S(1)} custom-call(s32[16]{0:T(128)S(1)} %multiply_add_fusion.idx, bf16[512,1024]{1,0:T(8,128)(2,1)} %collective-permute-done.4.refs_0_, bf16[512,1024]{1,0:T(8,128)(2,1)} %collective-permute-done.10.refs_1_, bf16[512,1024]{1,0:T(8,128)(2,1)} %collective-permute-done.13.refs_2_, ...), custom_call_target="tpu_custom_call" | custom-call | flops 6979321856 | bytes 13631488 | tf_op jit(solution)/shard_map/pallas_call | solution.py:170
  110.9 1.6 collective-permute-start.15
  113.0 1.5 collective-permute-start.17
  114.5 1.4 collective-permute-done.21.refs_0_.refs_4_
  115.9 1.5 collective-permute-done.22.refs_1_.refs_5_
  117.4 3.4 %collective-permute-done.15 = bf16[128,896]{1,0:T(8,128)(2,1)S(1)} collective-permute-done((bf16[128,896]{1,0:T(8,128)(2,1)S(1)}, bf16[128,896]{1,0:T(8,128)(2,1)S(1)}, u32[]{:S(2)}, u32[]{:S(2)}) %collective-permute-start.15) | collective-permute-done | bytes 229408 | tf_op jit(solution)/shard_map/ppermute | solution.py:25
  120.8 5.2 %collective-permute-done.16 = bf16[128,896]{1,0:T(8,128)(2,1)S(1)} collective-permute-done((bf16[128,896]{1,0:T(8,128)(2,1)S(1)}, bf16[128,896]{1,0:T(8,128)(2,1)S(1)}, u32[]{:S(2)}, u32[]{:S(2)}) %collective-permute-start.16) | collective-permute-done | bytes 229408 | tf_op jit(solution)/shard_map/ppermute | solution.py:25
  130.0 1.6 collective-permute-start.18
  131.6 2.6 collective-permute-start.19
  135.5 17.4 %shard_map.114.refs_8_ = f32[1664,256]{1,0:T(8,128)S(1)} custom-call(s32[16]{0:T(128)S(1)} %multiply_add_fusion.idx, bf16[256,2048]{1,0:T(8,128)(2,1)S(1)} %collective-permute-done.21.refs_0_.refs_4_, bf16[256,2048]{1,0:T(8,128)(2,1)} %collective-permute-done.22.refs_1_.refs_5_, ...), custom_call_target="tpu_custom_call", output_to_operand_aliasing={{}: (13, {})} | custom-call | flops 6979321856 | bytes 27262976 | tf_op jit(solution)/shard_map/pallas_call | solution.py:170
  158.8 1.5 collective-permute-start.26
  160.3 1.5 copy-done.7
  161.8 10.9 %shard_map.115 = bf16[256,896]{1,0:T(8,128)(2,1)S(1)} custom-call(s32[16]{0:T(128)S(1)} %multiply_add_fusion.idx, bf16[256,1024]{1,0:T(8,128)(2,1)} %collective-permute-done.27.refs_0_, bf16[256,1024]{1,0:T(8,128)(2,1)} %collective-permute-done.28.refs_1_, bf16[256,1024]{1,0:T(8,128)(2,1)S(1)} %collective-permute-done.29.refs_2_, ...), custom_call_target="tpu_custom_call" | custom-call | flops 3489660928 | bytes 13631488 | tf_op jit(solution)/shard_map/pallas_call | solution.py:170
  174.1 2.3 collective-permute-start.40
  176.4 4.7 %collective-permute-done.25.refs_1_ = bf16[512,896]{1,0:T(8,128)(2,1)} collective-permute-done((bf16[512,896]{1,0:T(8,128)(2,1)}, bf16[512,896]{1,0:T(8,128)(2,1)}, u32[]{:S(2)}, u32[]{:S(2)}) %collective-permute-start.25) | collective-permute-done | bytes 917536 | tf_op jit(solution)/shard_map/ppermute | solution.py:25
  183.4 2.3 collective-permute-start.31
  187.4 8.4 %collective-permute-done.31.refs_3_ = bf16[256,896]{1,0:T(8,128)(2,1)S(1)} collective-permute-done((bf16[256,896]{1,0:T(8,128)(2,1)S(1)}, bf16[256,896]{1,0:T(8,128)(2,1)S(1)}, u32[]{:S(2)}, u32[]{:S(2)}) %collective-permute-start.31) | collective-permute-done | bytes 458784 | tf_op jit(solution)/shard_map/ppermute | solution.py:25
  195.8 1.6 collective-permute-done.32.refs_4_
  199.8 2.7 collective-permute-start.46
  202.5 27.1 %shard_map.116 = bf16[512,2048]{1,0:T(8,128)(2,1)S(1)} custom-call(s32[8]{0:T(128)S(1)} %stack.74.idx, bf16[512,896]{1,0:T(8,128)(2,1)} %constant_dynamic-update-slice_fusion.refs_0_, bf16[512,896]{1,0:T(8,128)(2,1)} %collective-permute-done.25.refs_1_, bf16[512,896]{1,0:T(8,128)(2,1)} %collective-permute-done.26.refs_2_, ...), custom_call_target="tpu_custom_call" | custom-call | flops 13958643712 | bytes 27262976 | tf_op jit(solution)/shard_map/pallas_call | solution.py:237
  231.1 1.6 collective-permute-start.47
  233.2 10.4 %collective-permute-done.47.refs_1_ = bf16[256,896]{1,0:T(8,128)(2,1)S(1)} collective-permute-done((bf16[256,896]{1,0:T(8,128)(2,1)S(1)}, bf16[256,896]{1,0:T(8,128)(2,1)S(1)}, u32[]{:S(2)}, u32[]{:S(2)}) %collective-permute-start.47) | collective-permute-done | bytes 458784 | tf_op jit(solution)/shard_map/ppermute | solution.py:25
  246.7 4.5 %collective-permute-done.49.refs_3_ = bf16[128,896]{1,0:T(8,128)(2,1)S(1)} collective-permute-done((bf16[128,896]{1,0:T(8,128)(2,1)S(1)}, bf16[128,896]{1,0:T(8,128)(2,1)S(1)}, u32[]{:S(2)}, u32[]{:S(2)}) %collective-permute-start.49) | collective-permute-done | bytes 229408 | tf_op jit(solution)/shard_map/ppermute | solution.py:25
  252.7 1.4 collective-permute-start.42
  254.1 2.0 collective-permute-start.43
  256.1 18.0 %shard_map.117 = bf16[256,2048]{1,0:T(8,128)(2,1)S(1)} custom-call(s32[8]{0:T(128)S(1)} %stack.74.idx, bf16[256,896]{1,0:T(8,128)(2,1)S(1)} %constant_dynamic-update-slice_fusion.4.refs_0_, bf16[256,896]{1,0:T(8,128)(2,1)S(1)} %collective-permute-done.47.refs_1_, bf16[256,896]{1,0:T(8,128)(2,1)S(1)} %collective-permute-done.48.refs_2_, ...), custom_call_target="tpu_custom_call" | custom-call | flops 6979321856 | bytes 27262976 | tf_op jit(solution)/shard_map/pallas_call | solution.py:237
  274.3 1.5 collective-permute-start.57
  275.8 2.8 collective-permute-start.58
  278.6 12.6 %collective-permute-done.42 = bf16[128,2048]{1,0:T(8,128)(2,1)} collective-permute-done((bf16[128,2048]{1,0:T(8,128)(2,1)}, bf16[128,2048]{1,0:T(8,128)(2,1)}, u32[]{:S(2)}, u32[]{:S(2)}) %collective-permute-start.42) | collective-permute-done | bytes 524320 | tf_op jit(solution)/shard_map/ppermute | solution.py:31
  291.3 5.5 %collective-permute-done.56 = bf16[64,2048]{1,0:T(8,128)(2,1)S(1)} collective-permute-done((bf16[64,2048]{1,0:T(8,128)(2,1)S(1)}, bf16[64,2048]{1,0:T(8,128)(2,1)S(1)}, u32[]{:S(2)}, u32[]{:S(2)}) %collective-permute-start.56) | collective-permute-done | bytes 262176 | tf_op jit(solution)/shard_map/ppermute | solution.py:31
  296.8 21.8 %collective-permute-done.57 = bf16[64,2048]{1,0:T(8,128)(2,1)S(1)} collective-permute-done((bf16[64,2048]{1,0:T(8,128)(2,1)S(1)}, bf16[64,2048]{1,0:T(8,128)(2,1)S(1)}, u32[]{:S(2)}, u32[]{:S(2)}) %collective-permute-start.57) | collective-permute-done | bytes 262176 | tf_op jit(solution)/shard_map/ppermute | solution.py:31
  318.6 1.7 add_convert_fusion
  (179 shorter events, 37.4 us)
Async XLA Ops:
  5.1 15.3 %collective-permute-start.2 = (bf16[512,1024]{1,0:T(8,128)(2,1)}, bf16[512,1024]{1,0:T(8,128)(2,1)}, u32[]{:S(2)}, u32[]{:S(2)}) collective-permute-start(bf16[512,1024]{1,0:T(8,128)(2,1)} %fusion.4.refs_0_), channel_id=1, source_target_pairs={{0,4},{4,0},{8,12},{12,8},{16,20},{20,16},{24,28},{28,24},{1,5},{5... | collective-permute-start | bytes 3145736 | tf_op jit(solution)/shard_map/ppermute | solution.py:25
  5.6 29.5 %collective-permute-start = (bf16[512,1024]{1,0:T(8,128)(2,1)}, bf16[512,1024]{1,0:T(8,128)(2,1)}, u32[]{:S(2)}, u32[]{:S(2)}) collective-permute-start(bf16[512,1024]{1,0:T(8,128)(2,1)} %fusion.4.refs_0_), channel_id=1, source_target_pairs={{0,8},{4,12},{8,0},{12,4},{16,24},{20,28},{24,16},{28,20},{1,9},{5... | collective-permute-start | bytes 3145736 | tf_op jit(solution)/shard_map/ppermute | solution.py:25
  8.1 27.0 %collective-permute-start.1 = (bf16[512,1024]{1,0:T(8,128)(2,1)}, bf16[512,1024]{1,0:T(8,128)(2,1)}, u32[]{:S(2)}, u32[]{:S(2)}) collective-permute-start(bf16[512,1024]{1,0:T(8,128)(2,1)} %fusion.4.refs_0_), channel_id=1, source_target_pairs={{0,16},{4,20},{8,24},{12,28},{16,0},{20,4},{24,8},{28,12},{1,17},{... | collective-permute-start | bytes 3145736 | tf_op jit(solution)/shard_map/ppermute | solution.py:25
  11.9 8.6 %collective-permute-start.3 = (bf16[512,1024]{1,0:T(8,128)(2,1)}, bf16[512,1024]{1,0:T(8,128)(2,1)}, u32[]{:S(2)}, u32[]{:S(2)}) collective-permute-start(bf16[512,1024]{1,0:T(8,128)(2,1)} %fusion.7.refs_1_), channel_id=1, source_target_pairs={{0,4},{4,0},{8,12},{12,8},{16,20},{20,16},{24,28},{28,24},{1,5},{5... | collective-permute-start | bytes 3145736 | tf_op jit(solution)/shard_map/ppermute | solution.py:25
  16.6 19.7 %collective-permute-start.9 = (bf16[256,2048]{1,0:T(8,128)(2,1)}, bf16[256,2048]{1,0:T(8,128)(2,1)S(1)}, u32[]{:S(2)}, u32[]{:S(2)}) collective-permute-start(bf16[256,2048]{1,0:T(8,128)(2,1)} %convolution_convert_fusion.refs_0_.refs_1_), channel_id=1, source_target_pairs={{0,4},{4,0},{8,12},{12,8},{16,20},{20,16},{24,28},{28,24},{1,5},{5... | collective-permute-start | bytes 3145736 | tf_op jit(solution)/shard_map/ppermute | solution.py:25
  35.1 11.8 %collective-permute-start.7 = (bf16[512,1024]{1,0:T(8,128)(2,1)}, bf16[512,1024]{1,0:T(8,128)(2,1)S(1)}, u32[]{:S(2)}, u32[]{:S(2)}) collective-permute-start(bf16[512,1024]{1,0:T(8,128)(2,1)} %collective-permute-done.refs_0_), channel_id=1, source_target_pairs={{0,4},{4,0},{8,12},{12,8},{16,20},{20,16},{24,28},{28,24},{1,5},{5... | collective-permute-start | bytes 3145736 | tf_op jit(solution)/shard_map/ppermute | solution.py:25
  35.2 11.8 %collective-permute-start.8 = (bf16[512,1024]{1,0:T(8,128)(2,1)}, bf16[512,1024]{1,0:T(8,128)(2,1)S(1)}, u32[]{:S(2)}, u32[]{:S(2)}) collective-permute-start(bf16[512,1024]{1,0:T(8,128)(2,1)} %collective-permute-done.1.refs_1_), channel_id=1, source_target_pairs={{0,4},{4,0},{8,12},{12,8},{16,20},{20,16},{24,28},{28,24},{1,5},{5... | collective-permute-start | bytes 3145736 | tf_op jit(solution)/shard_map/ppermute | solution.py:25
  35.7 25.9 %collective-permute-start.5 = (bf16[512,1024]{1,0:T(8,128)(2,1)}, bf16[512,1024]{1,0:T(8,128)(2,1)S(1)}, u32[]{:S(2)}, u32[]{:S(2)}) collective-permute-start(bf16[512,1024]{1,0:T(8,128)(2,1)} %fusion.7.refs_1_), channel_id=1, source_target_pairs={{0,8},{4,12},{8,0},{12,4},{16,24},{20,28},{24,16},{28,20},{1,9},{5... | collective-permute-start | bytes 3145736 | tf_op jit(solution)/shard_map/ppermute | solution.py:25
  36.2 25.4 %collective-permute-start.6 = (bf16[512,1024]{1,0:T(8,128)(2,1)}, bf16[512,1024]{1,0:T(8,128)(2,1)S(1)}, u32[]{:S(2)}, u32[]{:S(2)}) collective-permute-start(bf16[512,1024]{1,0:T(8,128)(2,1)} %fusion.7.refs_1_), channel_id=1, source_target_pairs={{0,16},{4,20},{8,24},{12,28},{16,0},{20,4},{24,8},{28,12},{1,17},{... | collective-permute-start | bytes 3145736 | tf_op jit(solution)/shard_map/ppermute | solution.py:25
  62.2 25.7 %collective-permute-start.4 = (bf16[512,1024]{1,0:T(8,128)(2,1)}, bf16[512,1024]{1,0:T(8,128)(2,1)}, u32[]{:S(2)}, u32[]{:S(2)}) collective-permute-start(bf16[512,1024]{1,0:T(8,128)(2,1)} %collective-permute-done.refs_0_), channel_id=1, source_target_pairs={{0,16},{4,20},{8,24},{12,28},{16,0},{20,4},{24,8},{28,12},{1,17},{... | collective-permute-start | bytes 3145736 | tf_op jit(solution)/shard_map/ppermute | solution.py:25
  64.2 25.0 %collective-permute-start.10 = (bf16[512,1024]{1,0:T(8,128)(2,1)S(1)}, bf16[512,1024]{1,0:T(8,128)(2,1)}, u32[]{:S(2)}, u32[]{:S(2)}) collective-permute-start(bf16[512,1024]{1,0:T(8,128)(2,1)S(1)} %collective-permute-done.6.refs_1_), channel_id=1, source_target_pairs={{0,8},{4,12},{8,0},{12,4},{16,24},{20,28},{24,16},{28,20},{1,9},{5... | collective-permute-start | bytes 3145736 | tf_op jit(solution)/shard_map/ppermute | solution.py:25
  89.7 26.2 %collective-permute-start.21 = (bf16[256,2048]{1,0:T(8,128)(2,1)}, bf16[256,2048]{1,0:T(8,128)(2,1)S(1)}, u32[]{:S(2)}, u32[]{:S(2)}) collective-permute-start(bf16[256,2048]{1,0:T(8,128)(2,1)} %convolution_convert_fusion.refs_0_.refs_1_), channel_id=1, source_target_pairs={{0,8},{4,12},{8,0},{12,4},{16,24},{20,28},{24,16},{28,20},{1,9},{5... | collective-permute-start | bytes 3145736 | tf_op jit(solution)/shard_map/ppermute | solution.py:25
  91.2 26.3 %collective-permute-start.22 = (bf16[256,2048]{1,0:T(8,128)(2,1)}, bf16[256,2048]{1,0:T(8,128)(2,1)}, u32[]{:S(2)}, u32[]{:S(2)}) collective-permute-start(bf16[256,2048]{1,0:T(8,128)(2,1)} %convolution_convert_fusion.refs_0_.refs_1_), channel_id=1, source_target_pairs={{0,16},{4,20},{8,24},{12,28},{16,0},{20,4},{24,8},{28,12},{1,17},{... | collective-permute-start | bytes 3145736 | tf_op jit(solution)/shard_map/ppermute | solution.py:25
  110.9 9.9 %collective-permute-start.15 = (bf16[128,896]{1,0:T(8,128)(2,1)S(1)}, bf16[128,896]{1,0:T(8,128)(2,1)S(1)}, u32[]{:S(2)}, u32[]{:S(2)}) collective-permute-start(bf16[128,896]{1,0:T(8,128)(2,1)S(1)} %get-tuple-element.135), channel_id=1, source_target_pairs={{0,8},{4,12},{8,0},{12,4},{16,24},{20,28},{24,16},{28,20},{1,9},{5... | collective-permute-start | bytes 688136 | tf_op jit(solution)/shard_map/ppermute | solution.py:25
  112.5 13.5 %collective-permute-start.16 = (bf16[128,896]{1,0:T(8,128)(2,1)S(1)}, bf16[128,896]{1,0:T(8,128)(2,1)S(1)}, u32[]{:S(2)}, u32[]{:S(2)}) collective-permute-start(bf16[128,896]{1,0:T(8,128)(2,1)S(1)} %get-tuple-element.134), channel_id=1, source_target_pairs={{0,16},{4,20},{8,24},{12,28},{16,0},{20,4},{24,8},{28,12},{1,17},{... | collective-permute-start | bytes 688136 | tf_op jit(solution)/shard_map/ppermute | solution.py:25
  113.0 13.0 %collective-permute-start.17 = (bf16[128,896]{1,0:T(8,128)(2,1)S(1)}, bf16[128,896]{1,0:T(8,128)(2,1)S(1)}, u32[]{:S(2)}, u32[]{:S(2)}) collective-permute-start(bf16[128,896]{1,0:T(8,128)(2,1)S(1)} %get-tuple-element.133), channel_id=1, source_target_pairs={{0,24},{4,28},{8,16},{12,20},{16,8},{20,12},{24,0},{28,4},{1,25},{... | collective-permute-start | bytes 688136 | tf_op jit(solution)/shard_map/ppermute | solution.py:25
  126.8 7.4 %collective-permute-start.24 = (bf16[256,2048]{1,0:T(8,128)(2,1)}, bf16[256,2048]{1,0:T(8,128)(2,1)}, u32[]{:S(2)}, u32[]{:S(2)}) collective-permute-start(bf16[256,2048]{1,0:T(8,128)(2,1)} %collective-permute-done.22.refs_1_.refs_5_), channel_id=1, source_target_pairs={{0,4},{4,0},{8,12},{12,8},{16,20},{20,16},{24,28},{28,24},{1,5},{5... | collective-permute-start | bytes 3145736 | tf_op jit(solution)/shard_map/ppermute | solution.py:25
  128.4 25.7 %collective-permute-start.27 = (bf16[256,1024]{1,0:T(8,128)(2,1)S(1)}, bf16[256,1024]{1,0:T(8,128)(2,1)}, u32[]{:S(2)}, u32[]{:S(2)}) collective-permute-start(bf16[256,1024]{1,0:T(8,128)(2,1)S(1)} %slice.34), channel_id=1, source_target_pairs={{0,16},{4,20},{8,24},{12,28},{16,0},{20,4},{24,8},{28,12},{1,17},{... | collective-permute-start | bytes 1572872 | tf_op jit(solution)/shard_map/ppermute | solution.py:25
  129.0 25.2 %collective-permute-start.28 = (bf16[256,1024]{1,0:T(8,128)(2,1)S(1)}, bf16[256,1024]{1,0:T(8,128)(2,1)}, u32[]{:S(2)}, u32[]{:S(2)}) collective-permute-start(bf16[256,1024]{1,0:T(8,128)(2,1)S(1)} %slice.35), channel_id=1, source_target_pairs={{0,8},{4,12},{8,0},{12,4},{16,24},{20,28},{24,16},{28,20},{1,9},{5... | collective-permute-start | bytes 1572872 | tf_op jit(solution)/shard_map/ppermute | solution.py:25
  130.0 24.7 %collective-permute-start.18 = (bf16[128,896]{1,0:T(8,128)(2,1)S(1)}, bf16[128,896]{1,0:T(8,128)(2,1)S(1)}, u32[]{:S(2)}, u32[]{:S(2)}) collective-permute-start(bf16[128,896]{1,0:T(8,128)(2,1)S(1)} %get-tuple-element.130), channel_id=1, source_target_pairs={{0,1},{1,2},{2,3},{3,0},{4,5},{5,6},{6,7},{7,4},{8,9},{9,10},{10,1... | collective-permute-start | bytes 688136 | tf_op jit(solution)/shard_map/ppermute | solution.py:31
  131.6 23.1 %collective-permute-start.19 = (bf16[128,896]{1,0:T(8,128)(2,1)S(1)}, bf16[128,896]{1,0:T(8,128)(2,1)S(1)}, u32[]{:S(2)}, u32[]{:S(2)}) collective-permute-start(bf16[128,896]{1,0:T(8,128)(2,1)S(1)} %get-tuple-element.129), channel_id=1, source_target_pairs={{0,2},{1,3},{2,0},{3,1},{4,6},{5,7},{6,4},{7,5},{8,10},{9,11},{10,... | collective-permute-start | bytes 688136 | tf_op jit(solution)/shard_map/ppermute | solution.py:31
  134.2 20.5 %collective-permute-start.20 = (bf16[128,896]{1,0:T(8,128)(2,1)S(1)}, bf16[128,896]{1,0:T(8,128)(2,1)S(1)}, u32[]{:S(2)}, u32[]{:S(2)}) collective-permute-start(bf16[128,896]{1,0:T(8,128)(2,1)S(1)} %get-tuple-element.128), channel_id=1, source_target_pairs={{0,3},{1,0},{2,1},{3,2},{4,7},{5,4},{6,5},{7,6},{8,11},{9,8},{10,9... | collective-permute-start | bytes 688136 | tf_op jit(solution)/shard_map/ppermute | solution.py:31
  154.1 6.2 %collective-permute-start.29 = (bf16[256,1024]{1,0:T(8,128)(2,1)}, bf16[256,1024]{1,0:T(8,128)(2,1)S(1)}, u32[]{:S(2)}, u32[]{:S(2)}) collective-permute-start(bf16[256,1024]{1,0:T(8,128)(2,1)} %collective-permute-done.27.refs_0_), channel_id=1, source_target_pairs={{0,4},{4,0},{8,12},{12,8},{16,20},{20,16},{24,28},{28,24},{1,5},{5... | collective-permute-start | bytes 1572872 | tf_op jit(solution)/shard_map/ppermute | solution.py:25
  157.5 23.5 %collective-permute-start.25 = (bf16[512,896]{1,0:T(8,128)(2,1)}, bf16[512,896]{1,0:T(8,128)(2,1)}, u32[]{:S(2)}, u32[]{:S(2)}) collective-permute-start(bf16[512,896]{1,0:T(8,128)(2,1)} %constant_dynamic-update-slice_fusion.refs_0_), channel_id=1, source_target_pairs={{0,8},{4,12},{8,0},{12,4},{16,24},{20,28},{24,16},{28,20},{1,9},{5... | collective-permute-start | bytes 2752520 | tf_op jit(solution)/shard_map/ppermute | solution.py:25
  158.8 23.5 %collective-permute-start.26 = (bf16[512,896]{1,0:T(8,128)(2,1)}, bf16[512,896]{1,0:T(8,128)(2,1)}, u32[]{:S(2)}, u32[]{:S(2)}) collective-permute-start(bf16[512,896]{1,0:T(8,128)(2,1)} %constant_dynamic-update-slice_fusion.refs_0_), channel_id=1, source_target_pairs={{0,16},{4,20},{8,24},{12,28},{16,0},{20,4},{24,8},{28,12},{1,17},{... | collective-permute-start | bytes 2752520 | tf_op jit(solution)/shard_map/ppermute | solution.py:25
  172.8 13.9 %collective-permute-start.38 = (bf16[64,896]{1,0:T(8,128)(2,1)S(1)}, bf16[64,896]{1,0:T(8,128)(2,1)S(1)}, u32[]{:S(2)}, u32[]{:S(2)}) collective-permute-start(bf16[64,896]{1,0:T(8,128)(2,1)S(1)} %get-tuple-element.140), channel_id=1, source_target_pairs={{0,8},{4,12},{8,0},{12,4},{16,24},{20,28},{24,16},{28,20},{1,9},{5... | collective-permute-start | bytes 344072 | tf_op jit(solution)/shard_map/ppermute | solution.py:25
  173.4 13.4 %collective-permute-start.39 = (bf16[64,896]{1,0:T(8,128)(2,1)S(1)}, bf16[64,896]{1,0:T(8,128)(2,1)}, u32[]{:S(2)}, u32[]{:S(2)}) collective-permute-start(bf16[64,896]{1,0:T(8,128)(2,1)S(1)} %get-tuple-element.142), channel_id=1, source_target_pairs={{0,16},{4,20},{8,24},{12,28},{16,0},{20,4},{24,8},{28,12},{1,17},{... | collective-permute-start | bytes 344072 | tf_op jit(solution)/shard_map/ppermute | solution.py:25
  174.1 12.8 %collective-permute-start.40 = (bf16[64,896]{1,0:T(8,128)(2,1)S(1)}, bf16[64,896]{1,0:T(8,128)(2,1)}, u32[]{:S(2)}, u32[]{:S(2)}) collective-permute-start(bf16[64,896]{1,0:T(8,128)(2,1)S(1)} %get-tuple-element.141), channel_id=1, source_target_pairs={{0,24},{4,28},{8,16},{12,20},{16,8},{20,12},{24,0},{28,4},{1,25},{... | collective-permute-start | bytes 344072 | tf_op jit(solution)/shard_map/ppermute | solution.py:25
  181.0 17.5 %collective-permute-start.33 = (bf16[512,896]{1,0:T(8,128)(2,1)}, bf16[512,896]{1,0:T(8,128)(2,1)S(1)}, u32[]{:S(2)}, u32[]{:S(2)}) collective-permute-start(bf16[512,896]{1,0:T(8,128)(2,1)} %constant_dynamic-update-slice_fusion.refs_0_), channel_id=1, source_target_pairs={{0,4},{4,0},{8,12},{12,8},{16,20},{20,16},{24,28},{28,24},{1,5},{5... | collective-permute-start | bytes 2752520 | tf_op jit(solution)/shard_map/ppermute | solution.py:25
  183.4 12.4 %collective-permute-start.31 = (bf16[256,896]{1,0:T(8,128)(2,1)S(1)}, bf16[256,896]{1,0:T(8,128)(2,1)S(1)}, u32[]{:S(2)}, u32[]{:S(2)}) collective-permute-start(bf16[256,896]{1,0:T(8,128)(2,1)S(1)} %slice.36), channel_id=1, source_target_pairs={{0,16},{4,20},{8,24},{12,28},{16,0},{20,4},{24,8},{28,12},{1,17},{... | collective-permute-start | bytes 1376264 | tf_op jit(solution)/shard_map/ppermute | solution.py:25
  186.7 10.6 %collective-permute-start.32 = (bf16[256,896]{1,0:T(8,128)(2,1)S(1)}, bf16[256,896]{1,0:T(8,128)(2,1)}, u32[]{:S(2)}, u32[]{:S(2)}) collective-permute-start(bf16[256,896]{1,0:T(8,128)(2,1)S(1)} %slice.37), channel_id=1, source_target_pairs={{0,8},{4,12},{8,0},{12,4},{16,24},{20,28},{24,16},{28,20},{1,9},{5... | collective-permute-start | bytes 1376264 | tf_op jit(solution)/shard_map/ppermute | solution.py:25
  186.8 15.7 %collective-permute-start.34 = (bf16[512,896]{1,0:T(8,128)(2,1)}, bf16[512,896]{1,0:T(8,128)(2,1)S(1)}, u32[]{:S(2)}, u32[]{:S(2)}) collective-permute-start(bf16[512,896]{1,0:T(8,128)(2,1)} %collective-permute-done.25.refs_1_), channel_id=1, source_target_pairs={{0,4},{4,0},{8,12},{12,8},{16,20},{20,16},{24,28},{28,24},{1,5},{5... | collective-permute-start | bytes 2752520 | tf_op jit(solution)/shard_map/ppermute | solution.py:25
  186.9 15.6 %collective-permute-start.35 = (bf16[512,896]{1,0:T(8,128)(2,1)}, bf16[512,896]{1,0:T(8,128)(2,1)S(1)}, u32[]{:S(2)}, u32[]{:S(2)}) collective-permute-start(bf16[512,896]{1,0:T(8,128)(2,1)} %collective-permute-done.26.refs_2_), channel_id=1, source_target_pairs={{0,4},{4,0},{8,12},{12,8},{16,20},{20,16},{24,28},{28,24},{1,5},{5... | collective-permute-start | bytes 2752520 | tf_op jit(solution)/shard_map/ppermute | solution.py:25
  198.6 32.4 %collective-permute-start.44 = (bf16[64,896]{1,0:T(8,128)(2,1)S(1)}, bf16[64,896]{1,0:T(8,128)(2,1)S(1)}, u32[]{:S(2)}, u32[]{:S(2)}) collective-permute-start(bf16[64,896]{1,0:T(8,128)(2,1)S(1)} %get-tuple-element.138), channel_id=1, source_target_pairs={{0,1},{1,2},{2,3},{3,0},{4,5},{5,6},{6,7},{7,4},{8,9},{9,10},{10,1... | collective-permute-start | bytes 344072 | tf_op jit(solution)/shard_map/ppermute | solution.py:31
  199.3 31.7 %collective-permute-start.45 = (bf16[64,896]{1,0:T(8,128)(2,1)S(1)}, bf16[64,896]{1,0:T(8,128)(2,1)S(1)}, u32[]{:S(2)}, u32[]{:S(2)}) collective-permute-start(bf16[64,896]{1,0:T(8,128)(2,1)S(1)} %get-tuple-element.137), channel_id=1, source_target_pairs={{0,2},{1,3},{2,0},{3,1},{4,6},{5,7},{6,4},{7,5},{8,10},{9,11},{10,... | collective-permute-start | bytes 344072 | tf_op jit(solution)/shard_map/ppermute | solution.py:31
  199.8 31.2 %collective-permute-start.46 = (bf16[64,896]{1,0:T(8,128)(2,1)S(1)}, bf16[64,896]{1,0:T(8,128)(2,1)S(1)}, u32[]{:S(2)}, u32[]{:S(2)}) collective-permute-start(bf16[64,896]{1,0:T(8,128)(2,1)S(1)} %get-tuple-element.136), channel_id=1, source_target_pairs={{0,3},{1,0},{2,1},{3,2},{4,7},{5,4},{6,5},{7,6},{8,11},{9,8},{10,9... | collective-permute-start | bytes 344072 | tf_op jit(solution)/shard_map/ppermute | solution.py:31
  231.1 12.4 %collective-permute-start.47 = (bf16[256,896]{1,0:T(8,128)(2,1)S(1)}, bf16[256,896]{1,0:T(8,128)(2,1)S(1)}, u32[]{:S(2)}, u32[]{:S(2)}) collective-permute-start(bf16[256,896]{1,0:T(8,128)(2,1)S(1)} %constant_dynamic-update-slice_fusion.4.refs_0_), channel_id=1, source_target_pairs={{0,8},{4,12},{8,0},{12,4},{16,24},{20,28},{24,16},{28,20},{1,9},{5... | collective-permute-start | bytes 1376264 | tf_op jit(solution)/shard_map/ppermute | solution.py:25
  232.7 12.1 %collective-permute-start.48 = (bf16[256,896]{1,0:T(8,128)(2,1)S(1)}, bf16[256,896]{1,0:T(8,128)(2,1)S(1)}, u32[]{:S(2)}, u32[]{:S(2)}) collective-permute-start(bf16[256,896]{1,0:T(8,128)(2,1)S(1)} %constant_dynamic-update-slice_fusion.4.refs_0_), channel_id=1, source_target_pairs={{0,16},{4,20},{8,24},{12,28},{16,0},{20,4},{24,8},{28,12},{1,17},{... | collective-permute-start | bytes 1376264 | tf_op jit(solution)/shard_map/ppermute | solution.py:25
  233.2 18.5 %collective-permute-start.51 = (bf16[256,896]{1,0:T(8,128)(2,1)S(1)}, bf16[256,896]{1,0:T(8,128)(2,1)S(1)}, u32[]{:S(2)}, u32[]{:S(2)}) collective-permute-start(bf16[256,896]{1,0:T(8,128)(2,1)S(1)} %constant_dynamic-update-slice_fusion.4.refs_0_), channel_id=1, source_target_pairs={{0,4},{4,0},{8,12},{12,8},{16,20},{20,16},{24,28},{28,24},{1,5},{5... | collective-permute-start | bytes 1376264 | tf_op jit(solution)/shard_map/ppermute | solution.py:25
  244.8 6.4 %collective-permute-start.49 = (bf16[128,896]{1,0:T(8,128)(2,1)S(1)}, bf16[128,896]{1,0:T(8,128)(2,1)S(1)}, u32[]{:S(2)}, u32[]{:S(2)}) collective-permute-start(bf16[128,896]{1,0:T(8,128)(2,1)S(1)} %slice.38), channel_id=1, source_target_pairs={{0,16},{4,20},{8,24},{12,28},{16,0},{20,4},{24,8},{28,12},{1,17},{... | collective-permute-start | bytes 688136 | tf_op jit(solution)/shard_map/ppermute | solution.py:25
  246.2 9.9 %collective-permute-start.52 = (bf16[256,896]{1,0:T(8,128)(2,1)S(1)}, bf16[256,896]{1,0:T(8,128)(2,1)S(1)}, u32[]{:S(2)}, u32[]{:S(2)}) collective-permute-start(bf16[256,896]{1,0:T(8,128)(2,1)S(1)} %collective-permute-done.47.refs_1_), channel_id=1, source_target_pairs={{0,4},{4,0},{8,12},{12,8},{16,20},{20,16},{24,28},{28,24},{1,5},{5... | collective-permute-start | bytes 1376264 | tf_op jit(solution)/shard_map/ppermute | solution.py:25
  246.2 9.9 %collective-permute-start.53 = (bf16[256,896]{1,0:T(8,128)(2,1)S(1)}, bf16[256,896]{1,0:T(8,128)(2,1)S(1)}, u32[]{:S(2)}, u32[]{:S(2)}) collective-permute-start(bf16[256,896]{1,0:T(8,128)(2,1)S(1)} %collective-permute-done.48.refs_2_), channel_id=1, source_target_pairs={{0,4},{4,0},{8,12},{12,8},{16,20},{20,16},{24,28},{28,24},{1,5},{5... | collective-permute-start | bytes 1376264 | tf_op jit(solution)/shard_map/ppermute | solution.py:25
  251.7 24.1 %collective-permute-start.41 = (bf16[128,2048]{1,0:T(8,128)(2,1)}, bf16[128,2048]{1,0:T(8,128)(2,1)}, u32[]{:S(2)}, u32[]{:S(2)}) collective-permute-start(bf16[128,2048]{1,0:T(8,128)(2,1)} %get-tuple-element.122), channel_id=1, source_target_pairs={{0,1},{1,2},{2,3},{3,0},{4,5},{5,6},{6,7},{7,4},{8,9},{9,10},{10,1... | collective-permute-start | bytes 1572872 | tf_op jit(solution)/shard_map/ppermute | solution.py:31
  252.7 38.6 %collective-permute-start.42 = (bf16[128,2048]{1,0:T(8,128)(2,1)}, bf16[128,2048]{1,0:T(8,128)(2,1)}, u32[]{:S(2)}, u32[]{:S(2)}) collective-permute-start(bf16[128,2048]{1,0:T(8,128)(2,1)} %get-tuple-element.121), channel_id=1, source_target_pairs={{0,2},{1,3},{2,0},{3,1},{4,6},{5,7},{6,4},{7,5},{8,10},{9,11},{10,... | collective-permute-start | bytes 1572872 | tf_op jit(solution)/shard_map/ppermute | solution.py:31
  254.1 37.2 %collective-permute-start.43 = (bf16[128,2048]{1,0:T(8,128)(2,1)}, bf16[128,2048]{1,0:T(8,128)(2,1)}, u32[]{:S(2)}, u32[]{:S(2)}) collective-permute-start(bf16[128,2048]{1,0:T(8,128)(2,1)} %get-tuple-element.120), channel_id=1, source_target_pairs={{0,3},{1,0},{2,1},{3,2},{4,7},{5,4},{6,5},{7,6},{8,11},{9,8},{10,9... | collective-permute-start | bytes 1572872 | tf_op jit(solution)/shard_map/ppermute | solution.py:31
  274.2 22.6 %collective-permute-start.56 = (bf16[64,2048]{1,0:T(8,128)(2,1)S(1)}, bf16[64,2048]{1,0:T(8,128)(2,1)S(1)}, u32[]{:S(2)}, u32[]{:S(2)}) collective-permute-start(bf16[64,2048]{1,0:T(8,128)(2,1)S(1)} %get-tuple-element.126), channel_id=1, source_target_pairs={{0,1},{1,2},{2,3},{3,0},{4,5},{5,6},{6,7},{7,4},{8,9},{9,10},{10,1... | collective-permute-start | bytes 786440 | tf_op jit(solution)/shard_map/ppermute | solution.py:31
  274.3 44.3 %collective-permute-start.57 = (bf16[64,2048]{1,0:T(8,128)(2,1)S(1)}, bf16[64,2048]{1,0:T(8,128)(2,1)S(1)}, u32[]{:S(2)}, u32[]{:S(2)}) collective-permute-start(bf16[64,2048]{1,0:T(8,128)(2,1)S(1)} %get-tuple-element.125), channel_id=1, source_target_pairs={{0,2},{1,3},{2,0},{3,1},{4,6},{5,7},{6,4},{7,5},{8,10},{9,11},{10,... | collective-permute-start | bytes 786440 | tf_op jit(solution)/shard_map/ppermute | solution.py:31
  275.8 42.8 %collective-permute-start.58 = (bf16[64,2048]{1,0:T(8,128)(2,1)S(1)}, bf16[64,2048]{1,0:T(8,128)(2,1)S(1)}, u32[]{:S(2)}, u32[]{:S(2)}) collective-permute-start(bf16[64,2048]{1,0:T(8,128)(2,1)S(1)} %get-tuple-element.124), channel_id=1, source_target_pairs={{0,3},{1,0},{2,1},{3,2},{4,7},{5,4},{6,5},{7,6},{8,11},{9,8},{10,9... | collective-permute-start | bytes 786440 | tf_op jit(solution)/shard_map/ppermute | solution.py:31
  (31 other events, 166.3 us)
